TPU v7x, 512 devices: a whole 4x8x8 slice. The times are simulated.
512 devices in a mesh: prow: 16 (over y, core), pcol: 32 (over z, x).
Axes of the slice: x: 4, y: 8, z: 8, core: 2. Of those that a mesh axis runs over, the one named last changes fastest.
Arguments:
- right_side: float32 [6, 512, 2048], P(None, 'pcol', 'prow'), may hold values from -6 to 6
- coupling: float32 [2048, 2048], P('prow', 'pcol'), may hold values from -0.125 to 0.125
- row_bases: float32 [2048, 512], P('prow'), may hold values from -1 to 1, as said below
- row_values: float32 [4, 512], replicated, may hold values from 0.5 to 4
- column_bases: float32 [6, 512, 512], P(None, 'pcol'), may hold values from -1 to 1, as said below
- column_values: float32 [6, 512], replicated, may hold values from 0.5 to 4
- column_coupling: float32 [6, 512, 3072], P(None, 'pcol'), may hold values from -0.109375 to 0.109375
Outputs:
- solution: float32 [6, 512, 2048], P(None, 'pcol', 'prow')
Inputs may be any that keep to these rules, and one draw needn't show every extreme that they name: Each 512 x 512 block of row_bases is an orthogonal matrix. Each column_bases[j] is an orthogonal matrix.
All inputs are finite; a program needn't handle non-finite values.
Results may differ from a plain program's by a relative error of at most 0.00014.
Values sent between devices are 32-bit elements; how exact they have to be, the bound alone decides.
A program may use at most 64 MiB of HBM per device.

v0:
```python
import jax
import jax.numpy as jnp
from jax import lax
from jax.sharding import PartitionSpec as P

BS = 512
RB = 4
CB = 6
ROWS = 2048
STEPS = 9


HIGHEST = lax.Precision.HIGHEST


def joined_along(parts, dim):
    parts = jnp.moveaxis(parts, 0, dim)
    lengths = parts.shape
    return parts.reshape(*lengths[:dim], lengths[dim] * lengths[dim + 1], *lengths[dim + 2 :])


def gather_together(arrays, axis, dims):
    line = jnp.concatenate([a.reshape(-1) for a in arrays])
    lines, at, outs = (lax.all_gather(line, axis), 0, [])
    for a, dim in zip(arrays, dims):
        parts = lines[:, at : at + a.size].reshape(-1, *a.shape)
        outs.append(joined_along(parts, dim))
        at += a.size
    return tuple(outs)


def sent_to_all(shard, axis):
    copies = jnp.broadcast_to(shard, (lax.axis_size(axis), *shard.shape))
    return lax.all_to_all(copies, axis, split_axis=0, concat_axis=0, tiled=True)


def gather_directly(shard, axis, dim):
    parts = sent_to_all(shard, axis)
    return joined_along(parts, dim)


def swapped(block, axis, stride):
    count = lax.axis_size(axis)
    route = []
    for low in range(count):
        high = low | 1 << stride
        if high != low and high < count:
            route += [(low, high), (high, low)]
    return lax.ppermute(block, axis, route)


def contract(left, right, left_dim, right_dim):
    return lax.dot_general(
        left,
        right,
        (((left_dim,), (right_dim,)), ((), ())),
        precision=HIGHEST,
        preferred_element_type=jnp.float32,
    )


def select_block(array, position):
    return lax.dynamic_slice_in_dim(array, position, 1, 0)[0]


def shards(
    right_side, coupling, row_bases, row_values, column_bases, column_values, column_coupling
):
    panel, full_bases = gather_together((coupling, column_bases), "pcol", (1, 1))
    local_width = column_bases.shape[1]
    local_rows = right_side.shape[2]
    group_size = lax.axis_size("prow") // RB
    levels = group_size.bit_length() - 1
    prow_index = lax.axis_index("prow")
    pcol_index = lax.axis_index("pcol")
    own_block = prow_index // group_size
    own_values = select_block(row_values, own_block)
    block_ids = jnp.arange(CB, dtype=jnp.int32)
    row_blocks = jnp.arange(ROWS, dtype=jnp.int32) // BS

    def wave(wave_step, carried):
        solved, latest, pending, result = carried
        pieces = gather_directly(latest, "prow", 1)
        arrived = wave_step - RB + row_blocks
        placed = (block_ids[:, None] == arrived[None, :]).astype(jnp.float32)
        solved = solved + placed[:, None, :] * pieces[None, :, :]
        target = wave_step - (RB - 1 - own_block)
        active = jnp.logical_and(target >= 0, target < CB)
        column = jnp.clip(target, 0, CB - 1)
        source = select_block(right_side, column)
        upper_terms = contract(select_block(solved, column), panel, 1, 1)
        residual = source - upper_terms - select_block(pending, column)
        partial_value = contract(residual, row_bases, 1, 0)
        for bit_number in range(levels):
            partial_value = partial_value + swapped(partial_value, "prow", bit_number)
        column_basis = select_block(full_bases, column)
        shifts = select_block(column_values, column)
        gathered = gather_directly(partial_value, "pcol", 0)
        eigen_mix = contract(gathered, column_basis, 0, 0) / (own_values[:, None] + shifts[None, :])
        left_done = contract(row_bases, eigen_mix, 1, 0)
        full_block = contract(column_basis, left_done, 1, 1)
        fresh_block = lax.dynamic_slice_in_dim(full_block, pcol_index * local_width, local_width, 0)
        weight = active.astype(jnp.float32)
        fresh_block = fresh_block * weight
        couple = lax.dynamic_slice_in_dim(column_coupling, column * BS, BS, 2)
        later_terms = jnp.einsum("jbt,tr->jbr", couple, full_block, precision=HIGHEST)
        later_mask = (block_ids > column).astype(jnp.float32) * weight
        pending = pending + later_mask[:, None, None] * later_terms
        own_mask = (block_ids == column).astype(jnp.float32) * weight
        result = result + own_mask[:, None, None] * fresh_block[None, :, :]
        return (solved, fresh_block, pending, result)

    starting = (
        jnp.zeros((CB, local_width, ROWS), jnp.float32),
        jnp.zeros((local_width, local_rows), jnp.float32),
        jnp.zeros((CB, local_width, local_rows), jnp.float32),
        jnp.zeros((CB, local_width, local_rows), jnp.float32),
    )
    final_state = lax.fori_loop(0, STEPS, wave, starting)
    return final_state[3]


def solution(mesh):
    placed = (
        P(None, "pcol", "prow"),
        P("prow", "pcol"),
        P("prow", None),
        P(),
        P(None, "pcol", None),
        P(),
        P(None, "pcol", None),
    )
    return jax.shard_map(
        shards, mesh=mesh, in_specs=placed, out_specs=P(None, "pcol", "prow"), check_vma=False
    )
```

profile of v0, /device:TPU:1, one launch (start us, length us, event | category | flops | bytes accessed | tf_op | source)
XLA Modules:
  0.0 749.0 jit_solution(8711258020520480080)
XLA Ops:
  9.3 105.1 %all-gather.3.cloned.1.call-done = f32[1835008]{0:T(1024)} async-done(((f32[57344]{0:T(1024)}), f32[1835008]{0:T(1024)}) %all-gather.3.cloned.1.call-update) | async-done | bytes 7340048 | tf_op jit(solution)/shard_map/all_gather | solution.py:24
  114.4 6.9 reshape.88
  135.9 605.6 %while.23 = (s32[]{:T(128)}, f32[6,16,2048]{2,1,0:T(8,128)S(1)}, f32[16,128]{1,0:T(8,128)S(1)}, f32[6,16,128]{2,1,0:T(8,128)S(1)}, f32[6,16,128]{2,1,0:T(8,128)S...) while((s32[]{:T(128)}, f32[6,16,2048]{2,1,0:T(8,128)S(1)}, ...), condition=%wide.region_1.2_spmd.clone.clone, body=%wide.region_0.1_spmd.clone.clone.sunk | while | flops 2555586560 | bytes 15902294 | solution.py:119
  136.7 8.1 %all-to-all-start = ((f32[16,16,128]{2,1,0:T(8,128)}), f32[16,16,128]{2,1,0:T(8,128)S(1)}, u32[]{:S(2)}, u32[]{:S(2)}) async-start(f32[16,16,128]{2,1,0:T(8,128)} %broadcast_in_dim.52), calls=%async_computation | async-start | bytes 262144 | tf_op jit(solution)/shard_map/while/body/eval_jaxpr/all_to_all | solution.py:34
  144.9 8.8 %all-to-all-done = f32[16,16,128]{2,1,0:T(8,128)S(1)} async-done(((f32[16,16,128]{2,1,0:T(8,128)}), f32[16,16,128]{2,1,0:T(8,128)S(1)}, u32[]{:S(2)}, u32[]{:S(2)}) %all-to-all-start) | async-done | bytes 131104 | tf_op jit(solution)/shard_map/while/body/eval_jaxpr/all_to_all | solution.py:34
  170.7 25.1 %all-to-all-done.1 = f32[32,16,512]{2,1,0:T(8,128)S(1)} async-done(((f32[32,16,512]{2,1,0:T(8,128)}), f32[32,16,512]{2,1,0:T(8,128)S(1)}, u32[]{:S(2)}, u32[]{:S(2)}) %all-to-all-start.1) | async-done | bytes 1048608 | tf_op jit(solution)/shard_map/while/body/eval_jaxpr/all_to_all | solution.py:34
  211.6 9.1 %all-to-all-done = f32[16,16,128]{2,1,0:T(8,128)S(1)} async-done(((f32[16,16,128]{2,1,0:T(8,128)}), f32[16,16,128]{2,1,0:T(8,128)S(1)}, u32[]{:S(2)}, u32[]{:S(2)}) %all-to-all-start) | async-done | bytes 131104 | tf_op jit(solution)/shard_map/while/body/eval_jaxpr/all_to_all | solution.py:34
  237.9 25.1 %all-to-all-done.1 = f32[32,16,512]{2,1,0:T(8,128)S(1)} async-done(((f32[32,16,512]{2,1,0:T(8,128)}), f32[32,16,512]{2,1,0:T(8,128)S(1)}, u32[]{:S(2)}, u32[]{:S(2)}) %all-to-all-start.1) | async-done | bytes 1048608 | tf_op jit(solution)/shard_map/while/body/eval_jaxpr/all_to_all | solution.py:34
  272.2 6.5 all-to-all-start
  278.7 9.1 %all-to-all-done = f32[16,16,128]{2,1,0:T(8,128)S(1)} async-done(((f32[16,16,128]{2,1,0:T(8,128)}), f32[16,16,128]{2,1,0:T(8,128)S(1)}, u32[]{:S(2)}, u32[]{:S(2)}) %all-to-all-start) | async-done | bytes 131104 | tf_op jit(solution)/shard_map/while/body/eval_jaxpr/all_to_all | solution.py:34
  305.0 25.1 %all-to-all-done.1 = f32[32,16,512]{2,1,0:T(8,128)S(1)} async-done(((f32[32,16,512]{2,1,0:T(8,128)}), f32[32,16,512]{2,1,0:T(8,128)S(1)}, u32[]{:S(2)}, u32[]{:S(2)}) %all-to-all-start.1) | async-done | bytes 1048608 | tf_op jit(solution)/shard_map/while/body/eval_jaxpr/all_to_all | solution.py:34
  345.9 9.1 %all-to-all-done = f32[16,16,128]{2,1,0:T(8,128)S(1)} async-done(((f32[16,16,128]{2,1,0:T(8,128)}), f32[16,16,128]{2,1,0:T(8,128)S(1)}, u32[]{:S(2)}, u32[]{:S(2)}) %all-to-all-start) | async-done | bytes 131104 | tf_op jit(solution)/shard_map/while/body/eval_jaxpr/all_to_all | solution.py:34
  372.1 25.1 %all-to-all-done.1 = f32[32,16,512]{2,1,0:T(8,128)S(1)} async-done(((f32[32,16,512]{2,1,0:T(8,128)}), f32[32,16,512]{2,1,0:T(8,128)S(1)}, u32[]{:S(2)}, u32[]{:S(2)}) %all-to-all-start.1) | async-done | bytes 1048608 | tf_op jit(solution)/shard_map/while/body/eval_jaxpr/all_to_all | solution.py:34
  413.0 9.1 %all-to-all-done = f32[16,16,128]{2,1,0:T(8,128)S(1)} async-done(((f32[16,16,128]{2,1,0:T(8,128)}), f32[16,16,128]{2,1,0:T(8,128)S(1)}, u32[]{:S(2)}, u32[]{:S(2)}) %all-to-all-start) | async-done | bytes 131104 | tf_op jit(solution)/shard_map/while/body/eval_jaxpr/all_to_all | solution.py:34
  439.3 25.1 %all-to-all-done.1 = f32[32,16,512]{2,1,0:T(8,128)S(1)} async-done(((f32[32,16,512]{2,1,0:T(8,128)}), f32[32,16,512]{2,1,0:T(8,128)S(1)}, u32[]{:S(2)}, u32[]{:S(2)}) %all-to-all-start.1) | async-done | bytes 1048608 | tf_op jit(solution)/shard_map/while/body/eval_jaxpr/all_to_all | solution.py:34
  480.2 9.1 %all-to-all-done = f32[16,16,128]{2,1,0:T(8,128)S(1)} async-done(((f32[16,16,128]{2,1,0:T(8,128)}), f32[16,16,128]{2,1,0:T(8,128)S(1)}, u32[]{:S(2)}, u32[]{:S(2)}) %all-to-all-start) | async-done | bytes 131104 | tf_op jit(solution)/shard_map/while/body/eval_jaxpr/all_to_all | solution.py:34
  506.4 25.1 %all-to-all-done.1 = f32[32,16,512]{2,1,0:T(8,128)S(1)} async-done(((f32[32,16,512]{2,1,0:T(8,128)}), f32[32,16,512]{2,1,0:T(8,128)S(1)}, u32[]{:S(2)}, u32[]{:S(2)}) %all-to-all-start.1) | async-done | bytes 1048608 | tf_op jit(solution)/shard_map/while/body/eval_jaxpr/all_to_all | solution.py:34
  547.3 9.1 %all-to-all-done = f32[16,16,128]{2,1,0:T(8,128)S(1)} async-done(((f32[16,16,128]{2,1,0:T(8,128)}), f32[16,16,128]{2,1,0:T(8,128)S(1)}, u32[]{:S(2)}, u32[]{:S(2)}) %all-to-all-start) | async-done | bytes 131104 | tf_op jit(solution)/shard_map/while/body/eval_jaxpr/all_to_all | solution.py:34
  573.5 25.1 %all-to-all-done.1 = f32[32,16,512]{2,1,0:T(8,128)S(1)} async-done(((f32[32,16,512]{2,1,0:T(8,128)}), f32[32,16,512]{2,1,0:T(8,128)S(1)}, u32[]{:S(2)}, u32[]{:S(2)}) %all-to-all-start.1) | async-done | bytes 1048608 | tf_op jit(solution)/shard_map/while/body/eval_jaxpr/all_to_all | solution.py:34
  607.9 6.5 all-to-all-start
  614.4 9.1 %all-to-all-done = f32[16,16,128]{2,1,0:T(8,128)S(1)} async-done(((f32[16,16,128]{2,1,0:T(8,128)}), f32[16,16,128]{2,1,0:T(8,128)S(1)}, u32[]{:S(2)}, u32[]{:S(2)}) %all-to-all-start) | async-done | bytes 131104 | tf_op jit(solution)/shard_map/while/body/eval_jaxpr/all_to_all | solution.py:34
  640.7 25.1 %all-to-all-done.1 = f32[32,16,512]{2,1,0:T(8,128)S(1)} async-done(((f32[32,16,512]{2,1,0:T(8,128)}), f32[32,16,512]{2,1,0:T(8,128)S(1)}, u32[]{:S(2)}, u32[]{:S(2)}) %all-to-all-start.1) | async-done | bytes 1048608 | tf_op jit(solution)/shard_map/while/body/eval_jaxpr/all_to_all | solution.py:34
  681.5 9.1 %all-to-all-done = f32[16,16,128]{2,1,0:T(8,128)S(1)} async-done(((f32[16,16,128]{2,1,0:T(8,128)}), f32[16,16,128]{2,1,0:T(8,128)S(1)}, u32[]{:S(2)}, u32[]{:S(2)}) %all-to-all-start) | async-done | bytes 131104 | tf_op jit(solution)/shard_map/while/body/eval_jaxpr/all_to_all | solution.py:34
  707.8 25.1 %all-to-all-done.1 = f32[32,16,512]{2,1,0:T(8,128)S(1)} async-done(((f32[32,16,512]{2,1,0:T(8,128)}), f32[32,16,512]{2,1,0:T(8,128)S(1)}, u32[]{:S(2)}, u32[]{:S(2)}) %all-to-all-start.1) | async-done | bytes 1048608 | tf_op jit(solution)/shard_map/while/body/eval_jaxpr/all_to_all | solution.py:34
  (257 shorter events, 293.4 us)
Async XLA Ops:
  6.5 107.8 %all-gather.3.cloned.1.call-start = ((), (), s32[]{:S(2)}) async-start(), calls=%async_computation.2 | async-start | bytes 7569408 | tf_op jit(solution)/shard_map/all_gather | solution.py:24
  136.7 17.0 %all-to-all-start = ((f32[16,16,128]{2,1,0:T(8,128)}), f32[16,16,128]{2,1,0:T(8,128)S(1)}, u32[]{:S(2)}, u32[]{:S(2)}) async-start(f32[16,16,128]{2,1,0:T(8,128)} %broadcast_in_dim.52), calls=%async_computation | async-start | bytes 262144 | tf_op jit(solution)/shard_map/while/body/eval_jaxpr/all_to_all | solution.py:34
  158.9 4.6 collective-permute-start.1
  164.7 31.1 %all-to-all-start.1 = ((f32[32,16,512]{2,1,0:T(8,128)}), f32[32,16,512]{2,1,0:T(8,128)S(1)}, u32[]{:S(2)}, u32[]{:S(2)}) async-start(f32[32,16,512]{2,1,0:T(8,128)} %broadcast_in_dim.53), calls=%async_computation.1 | async-start | bytes 2097152 | tf_op jit(solution)/shard_map/while/body/eval_jaxpr/all_to_all | solution.py:34
  205.1 15.6 %all-to-all-start = ((f32[16,16,128]{2,1,0:T(8,128)}), f32[16,16,128]{2,1,0:T(8,128)S(1)}, u32[]{:S(2)}, u32[]{:S(2)}) async-start(f32[16,16,128]{2,1,0:T(8,128)} %broadcast_in_dim.52), calls=%async_computation | async-start | bytes 262144 | tf_op jit(solution)/shard_map/while/body/eval_jaxpr/all_to_all | solution.py:34
  226.0 4.6 collective-permute-start.1
  231.8 31.2 %all-to-all-start.1 = ((f32[32,16,512]{2,1,0:T(8,128)}), f32[32,16,512]{2,1,0:T(8,128)S(1)}, u32[]{:S(2)}, u32[]{:S(2)}) async-start(f32[32,16,512]{2,1,0:T(8,128)} %broadcast_in_dim.53), calls=%async_computation.1 | async-start | bytes 2097152 | tf_op jit(solution)/shard_map/while/body/eval_jaxpr/all_to_all | solution.py:34
  272.2 15.6 %all-to-all-start = ((f32[16,16,128]{2,1,0:T(8,128)}), f32[16,16,128]{2,1,0:T(8,128)S(1)}, u32[]{:S(2)}, u32[]{:S(2)}) async-start(f32[16,16,128]{2,1,0:T(8,128)} %broadcast_in_dim.52), calls=%async_computation | async-start | bytes 262144 | tf_op jit(solution)/shard_map/while/body/eval_jaxpr/all_to_all | solution.py:34
  298.9 31.2 %all-to-all-start.1 = ((f32[32,16,512]{2,1,0:T(8,128)}), f32[32,16,512]{2,1,0:T(8,128)S(1)}, u32[]{:S(2)}, u32[]{:S(2)}) async-start(f32[32,16,512]{2,1,0:T(8,128)} %broadcast_in_dim.53), calls=%async_computation.1 | async-start | bytes 2097152 | tf_op jit(solution)/shard_map/while/body/eval_jaxpr/all_to_all | solution.py:34
  339.4 15.6 %all-to-all-start = ((f32[16,16,128]{2,1,0:T(8,128)}), f32[16,16,128]{2,1,0:T(8,128)S(1)}, u32[]{:S(2)}, u32[]{:S(2)}) async-start(f32[16,16,128]{2,1,0:T(8,128)} %broadcast_in_dim.52), calls=%async_computation | async-start | bytes 262144 | tf_op jit(solution)/shard_map/while/body/eval_jaxpr/all_to_all | solution.py:34
  360.3 4.6 collective-permute-start.1
  366.1 31.2 %all-to-all-start.1 = ((f32[32,16,512]{2,1,0:T(8,128)}), f32[32,16,512]{2,1,0:T(8,128)S(1)}, u32[]{:S(2)}, u32[]{:S(2)}) async-start(f32[32,16,512]{2,1,0:T(8,128)} %broadcast_in_dim.53), calls=%async_computation.1 | async-start | bytes 2097152 | tf_op jit(solution)/shard_map/while/body/eval_jaxpr/all_to_all | solution.py:34
  406.5 15.6 %all-to-all-start = ((f32[16,16,128]{2,1,0:T(8,128)}), f32[16,16,128]{2,1,0:T(8,128)S(1)}, u32[]{:S(2)}, u32[]{:S(2)}) async-start(f32[16,16,128]{2,1,0:T(8,128)} %broadcast_in_dim.52), calls=%async_computation | async-start | bytes 262144 | tf_op jit(solution)/shard_map/while/body/eval_jaxpr/all_to_all | solution.py:34
  427.4 4.6 collective-permute-start.1
  433.2 31.2 %all-to-all-start.1 = ((f32[32,16,512]{2,1,0:T(8,128)}), f32[32,16,512]{2,1,0:T(8,128)S(1)}, u32[]{:S(2)}, u32[]{:S(2)}) async-start(f32[32,16,512]{2,1,0:T(8,128)} %broadcast_in_dim.53), calls=%async_computation.1 | async-start | bytes 2097152 | tf_op jit(solution)/shard_map/while/body/eval_jaxpr/all_to_all | solution.py:34
  473.6 15.6 %all-to-all-start = ((f32[16,16,128]{2,1,0:T(8,128)}), f32[16,16,128]{2,1,0:T(8,128)S(1)}, u32[]{:S(2)}, u32[]{:S(2)}) async-start(f32[16,16,128]{2,1,0:T(8,128)} %broadcast_in_dim.52), calls=%async_computation | async-start | bytes 262144 | tf_op jit(solution)/shard_map/while/body/eval_jaxpr/all_to_all | solution.py:34
  500.3 31.2 %all-to-all-start.1 = ((f32[32,16,512]{2,1,0:T(8,128)}), f32[32,16,512]{2,1,0:T(8,128)S(1)}, u32[]{:S(2)}, u32[]{:S(2)}) async-start(f32[32,16,512]{2,1,0:T(8,128)} %broadcast_in_dim.53), calls=%async_computation.1 | async-start | bytes 2097152 | tf_op jit(solution)/shard_map/while/body/eval_jaxpr/all_to_all | solution.py:34
  540.8 15.6 %all-to-all-start = ((f32[16,16,128]{2,1,0:T(8,128)}), f32[16,16,128]{2,1,0:T(8,128)S(1)}, u32[]{:S(2)}, u32[]{:S(2)}) async-start(f32[16,16,128]{2,1,0:T(8,128)} %broadcast_in_dim.52), calls=%async_computation | async-start | bytes 262144 | tf_op jit(solution)/shard_map/while/body/eval_jaxpr/all_to_all | solution.py:34
  567.5 31.2 %all-to-all-start.1 = ((f32[32,16,512]{2,1,0:T(8,128)}), f32[32,16,512]{2,1,0:T(8,128)S(1)}, u32[]{:S(2)}, u32[]{:S(2)}) async-start(f32[32,16,512]{2,1,0:T(8,128)} %broadcast_in_dim.53), calls=%async_computation.1 | async-start | bytes 2097152 | tf_op jit(solution)/shard_map/while/body/eval_jaxpr/all_to_all | solution.py:34
  607.9 15.6 %all-to-all-start = ((f32[16,16,128]{2,1,0:T(8,128)}), f32[16,16,128]{2,1,0:T(8,128)S(1)}, u32[]{:S(2)}, u32[]{:S(2)}) async-start(f32[16,16,128]{2,1,0:T(8,128)} %broadcast_in_dim.52), calls=%async_computation | async-start | bytes 262144 | tf_op jit(solution)/shard_map/while/body/eval_jaxpr/all_to_all | solution.py:34
  628.8 4.6 collective-permute-start.1
  634.6 31.2 %all-to-all-start.1 = ((f32[32,16,512]{2,1,0:T(8,128)}), f32[32,16,512]{2,1,0:T(8,128)S(1)}, u32[]{:S(2)}, u32[]{:S(2)}) async-start(f32[32,16,512]{2,1,0:T(8,128)} %broadcast_in_dim.53), calls=%async_computation.1 | async-start | bytes 2097152 | tf_op jit(solution)/shard_map/while/body/eval_jaxpr/all_to_all | solution.py:34
  675.0 15.6 %all-to-all-start = ((f32[16,16,128]{2,1,0:T(8,128)}), f32[16,16,128]{2,1,0:T(8,128)S(1)}, u32[]{:S(2)}, u32[]{:S(2)}) async-start(f32[16,16,128]{2,1,0:T(8,128)} %broadcast_in_dim.52), calls=%async_computation | async-start | bytes 262144 | tf_op jit(solution)/shard_map/while/body/eval_jaxpr/all_to_all | solution.py:34
  701.7 31.2 %all-to-all-start.1 = ((f32[32,16,512]{2,1,0:T(8,128)}), f32[32,16,512]{2,1,0:T(8,128)S(1)}, u32[]{:S(2)}, u32[]{:S(2)}) async-start(f32[32,16,512]{2,1,0:T(8,128)} %broadcast_in_dim.53), calls=%async_computation.1 | async-start | bytes 2097152 | tf_op jit(solution)/shard_map/while/body/eval_jaxpr/all_to_all | solution.py:34
  (18 other events, 60.8 us)
Sparse Core Ops, SparseCore 0:
  10.5 103.8 all-gather.2
where the time goes:
time: 755 us; the launch traced here: 749 us
  waiting for transfers between devices  448 us (59%)
  starting transfers between devices  142 us (19%)
  matrix products  93.4 us (12%)
  local copies, waits for them, and re-layouts  46.7 us (6%)
  between operations  13.5 us (2%)
    all_to_all x18, waiting for transfers between devices, sent_to_all(): return lax.all_to_all(copies, axis, split_axis=0, concat_axis=0, tiled=True)  308 us
    all_to_all x18, starting transfers between devices, sent_to_all(): return lax.all_to_all(copies, axis, split_axis=0, concat_axis=0, tiled=True)  107 us
    all_gather x1, waiting for transfers between devices, gather_together(): lines, at, outs = (lax.all_gather(line, axis), 0, [])  105 us
    dot_general x45, matrix products, contract(): lax.dot_general(left, right, (((left_dim,), (right_dim,)), ((), ())), pre...  82 us
    ppermute x18, waiting for transfers between devices, swapped(): return lax.ppermute(block, axis, route)  34.9 us
    ppermute x18, starting transfers between devices, swapped(): return lax.ppermute(block, axis, route)  34.7 us
    broadcast_in_dim x18, local copies, waits for them, and re-layouts, sent_to_all(): copies = jnp.broadcast_to(shard, (lax.axis_size(axis), *shard.shape))  16 us
  transfers between devices with their start and end apart: 37, of which 37 were waited for; matrix products, arithmetic and copies ran while one was open for 1% of the time, Pallas kernels for 0%

commit v1 on v0

v1 whole, which is shorter than its diff:
```python
import functools

import jax
import jax.numpy as jnp
from jax import lax
from jax.experimental import pallas as pl
from jax.experimental.pallas import tpu as pltpu
from jax.sharding import PartitionSpec as P

RB = 4
CB = 6
HIGHEST = lax.Precision.HIGHEST
MESH = pl.DeviceIdType.MESH
F32 = jnp.float32
BF16 = jnp.bfloat16


def halves(value):
    high = value.astype(BF16)
    low = (value - high.astype(F32)).astype(BF16)
    return high, low


def dot_of(left, right, dims):
    return lax.dot_general(left, right, (dims, ((), ())), preferred_element_type=F32)


def dot_split(left, right, dims):
    (left_high, left_low), (right_high, right_low) = left, right
    small = dot_of(left_low, right_high, dims) + dot_of(left_high, right_low, dims)
    return dot_of(left_high, right_high, dims) + small


def waves(
    np_, nq, cw, at, lhs, den, bases, out, yown, wown, yrow, ycol, wbuf, pend, acc, sems
):
    ns = nq // RB
    fw, ew = cw.shape[1], cw.shape[2]
    bs = fw * np_
    q = lax.axis_index("prow")
    p = lax.axis_index("pcol")
    i = q // ns
    s = q % ns
    row_send, row_recv, col_send, col_recv, w_send, w_recv = (sems.at[n] for n in range(6))

    barrier = pltpu.get_barrier_semaphore()

    @pl.loop(1, np_)
    def _(d):
        pl.semaphore_signal(barrier, inc=1, device_id=(q, (p + d) % np_), device_id_type=MESH)

    @pl.loop(1, nq)
    def _(d):
        pl.semaphore_signal(barrier, inc=1, device_id=((q + d) % nq, p), device_id_type=MESH)

    pl.semaphore_wait(barrier, np_ + nq - 2)

    pend[...] = cw[...]
    own_rows = pl.ds(pl.multiple_of(p * fw, fw), fw)
    own_lanes = pl.ds(pl.multiple_of(s * ew, ew), ew)

    for j in range(CB):
        acc[...] = pend[j]
        for k in range(1, RB):

            @pl.when(k > i)
            def _(k=k):
                pltpu.make_async_copy(
                    ycol.at[k - 1, j], ycol.at[k - 1, j], col_recv.at[(k - 1) * CB + j]
                ).wait()
                term = dot_split(
                    halves(ycol[k - 1, j]), halves(at[(k - 1) * bs : k * bs]), ((1,), (0,))
                )
                acc[...] -= term

        yown[j] = acc[...] / den[j]
        yrow[j, own_rows, :] = yown[j]

        @pl.loop(1, np_)
        def _(d):
            pltpu.make_async_remote_copy(
                src_ref=yown.at[j],
                dst_ref=yrow.at[j, own_rows],
                send_sem=row_send.at[j],
                recv_sem=row_recv.at[j],
                device_id=(q, (p + d) % np_),
                device_id_type=MESH,
            ).start()

        for k in range(1, RB):

            @pl.when(i == k)
            def _(k=k):
                @pl.loop(0, k * ns)
                def _(target):
                    pltpu.make_async_remote_copy(
                        src_ref=yown.at[j],
                        dst_ref=ycol.at[k - 1, j, :, own_lanes],
                        send_sem=col_send.at[j],
                        recv_sem=col_recv.at[(k - 1) * CB + j],
                        device_id=(target, p),
                        device_id_type=MESH,
                    ).start()

        arrived = yrow.at[j, pl.ds(0, bs - fw)]
        pltpu.make_async_copy(arrived, arrived, row_recv.at[j]).wait()
        rows = (CB - j) * fw
        both = dot_split(halves(lhs[j, :rows]), halves(yrow[j]), ((1,), (0,)))
        wown[j] = both[:fw]
        for later in range(j + 1, CB):
            at_row = (later - j) * fw
            pend[later] -= both[at_row : at_row + fw]
        wbuf[j, :, own_lanes] = wown[j]

        @pl.loop(1, ns)
        def _(d):
            pltpu.make_async_remote_copy(
                src_ref=wown.at[j],
                dst_ref=wbuf.at[j, :, own_lanes],
                send_sem=w_send.at[j],
                recv_sem=w_recv.at[j],
                device_id=(i * ns + (s + d) % ns, p),
                device_id_type=MESH,
            ).start()

    bases_split = halves(bases[...])
    for j in range(CB):
        part = wbuf.at[j, :, pl.ds(0, (ns - 1) * ew)]
        pltpu.make_async_copy(part, part, w_recv.at[j]).wait()
        out[j] = dot_split(halves(wbuf[j]), bases_split, ((1,), (1,)))

    for j in range(CB):
        arrived = yrow.at[j, pl.ds(0, bs - fw)]
        pltpu.make_async_copy(arrived, arrived, row_send.at[j]).wait()
        part = wbuf.at[j, :, pl.ds(0, (ns - 1) * ew)]
        pltpu.make_async_copy(part, part, w_send.at[j]).wait()
        for k in range(1, RB):

            @pl.when(i == k)
            def _(k=k):
                sent = yrow.at[j, pl.ds(0, fw * k * ns)]
                pltpu.make_async_copy(sent, sent, col_send.at[j]).wait()


def run_waves(np_, nq, cw, at, lhs, den, bases):
    fw, ew = cw.shape[1], cw.shape[2]
    bs = fw * np_
    vmem = pl.BlockSpec(memory_space=pltpu.VMEM)
    return pl.pallas_call(
        functools.partial(waves, np_, nq),
        out_shape=jax.ShapeDtypeStruct((CB, fw, ew), F32),
        in_specs=[vmem] * 5,
        out_specs=vmem,
        scratch_shapes=[
            pltpu.VMEM((CB, fw, ew), F32),
            pltpu.VMEM((CB, fw, ew), F32),
            pltpu.VMEM((CB, bs, ew), F32),
            pltpu.VMEM((RB - 1, CB, fw, bs), F32),
            pltpu.VMEM((CB, fw, bs), F32),
            pltpu.VMEM((CB, fw, ew), F32),
            pltpu.VMEM((fw, ew), F32),
            pltpu.SemaphoreType.DMA((6, (RB - 1) * CB)),
        ],
        compiler_params=pltpu.CompilerParams(collective_id=0, has_side_effects=True),
    )(cw, at, lhs, den, bases)


def take(array, index):
    return lax.dynamic_index_in_dim(array, index, 0, keepdims=False)


def product(spec, left, right):
    return jnp.einsum(spec, left, right, precision=HIGHEST, preferred_element_type=F32)


def shards(np_, nq, right_side, coupling, row_bases, row_values, column_bases, column_values, column_coupling):
    ns = nq // RB
    fw, ew = right_side.shape[1], right_side.shape[2]
    bs = row_bases.shape[1]
    q = lax.axis_index("prow")
    p = lax.axis_index("pcol")
    i, s = q // ns, q % ns
    groups = [[g * ns + m for m in range(ns)] for g in range(RB)]
    cw_width = coupling.shape[1]
    nw = bs // cw_width
    blocks = [[g * nw + m for m in range(nw)] for g in range(np_ // nw)]

    half = product("jbr,re->jbe", right_side, row_bases)
    half = lax.psum_scatter(half, "prow", scatter_dimension=2, axis_index_groups=groups, tiled=True)
    full = product("jbf,jbe->jfe", column_bases, half)
    cw = lax.psum_scatter(full, "pcol", scatter_dimension=1, tiled=True)

    inner = product("rc,re->ce", coupling, row_bases)
    inner = lax.psum_scatter(inner, "prow", scatter_dimension=1, axis_index_groups=groups, tiled=True)
    per_row = ew // cw_width
    piece = lax.dynamic_slice_in_dim(row_bases, (p % per_row) * cw_width, cw_width, 0)
    piece = lax.psum(jnp.where(q == p // per_row, piece, 0.0), "prow")
    outer = product("ce,cg->eg", piece, inner)
    outer = lax.psum_scatter(outer, "pcol", scatter_dimension=0, axis_index_groups=blocks, tiled=True)
    at = lax.all_gather(outer, "pcol", axis=0, tiled=True)[bs:]

    pairs = [(l, j) for j in range(1, CB) for l in range(j)]
    of_l = jnp.array([l for l, j in pairs] + [0], jnp.int32)
    of_j = jnp.array([j for l, j in pairs] + [0], jnp.int32)
    l_at, j_at = of_l[q], of_j[q]
    basis = lax.all_gather(take(column_bases, l_at), "pcol", axis=0, tiled=True)
    mine = lax.dynamic_slice_in_dim(take(column_coupling, j_at), l_at * bs, bs, 1)
    mixed = product("bt,tf->bf", mine, basis)
    mixed = product("bg,bf->gf", take(column_bases, j_at), mixed)
    mixed = lax.psum_scatter(mixed, "pcol", scatter_dimension=0, tiled=True)
    mixed = lax.all_gather(mixed, "prow", axis=0)
    lhs = []
    for l in range(CB):
        rows = [column_bases[l]] + [mixed[pairs.index((l, j))] for j in range(l + 1, CB)]
        rows += [jnp.zeros((l * fw, bs), F32)] if l else []
        lhs.append(jnp.concatenate(rows, 0))
    lhs = jnp.stack(lhs)

    own_values = lax.dynamic_slice(row_values, (i, s * ew), (1, ew))
    own_shifts = lax.dynamic_slice_in_dim(column_values, p * fw, fw, 1)
    den = own_shifts[:, :, None] + own_values[:, None, :]
    return run_waves(np_, nq, cw, at, lhs, den, row_bases)


def solution(mesh):
    placed = (
        P(None, "pcol", "prow"),
        P("prow", "pcol"),
        P("prow", None),
        P(),
        P(None, "pcol", None),
        P(),
        P(None, "pcol", None),
    )
    body = functools.partial(shards, mesh.shape["pcol"], mesh.shape["prow"])
    return jax.shard_map(
        body, mesh=mesh, in_specs=placed, out_specs=P(None, "pcol", "prow"), check_vma=False
    )
```

time: 755 us -> 769 us (1.019)
  waiting for transfers between devices: 448 us -> 607 us
  starting transfers between devices: 142 us -> 0.33 us
  Pallas kernels: 0 us -> 94.8 us
  matrix products: 93.4 us -> 13.5 us
  local copies, waits for them, and re-layouts: 46.7 us -> 7.07 us
  blocking collectives: 0 us -> 24.5 us
    reduce_scatter x0 -> x5, waiting for transfers between devices: none -> 376 us  [the longest x1 201 us: shards(): cw = lax.psum_scatter(full, 'pcol', scatter_dimension=1, tiled=True)]
    all_to_all x18 -> x0, waiting for transfers between devices: 308 us -> none  [sent_to_all(): return lax.all_to_all(copies, axis, split_axis=0, concat_axis=0, tiled=True)]
    psum x0 -> x1, waiting for transfers between devices: none -> 120 us  [shards(): piece = lax.psum(jnp.where(q == p // per_row, piece, 0.0), 'prow')]
    all_to_all x18 -> x0, starting transfers between devices: 107 us -> none  [sent_to_all(): return lax.all_to_all(copies, axis, split_axis=0, concat_axis=0, tiled=True)]
    pallas_call x0 -> x1, Pallas kernels: none -> 94.8 us  [run_waves(): pl.pallas_call(functools.partial(waves, np_, nq), out_shape=jax.ShapeDtyp...]
    dot_general x54 -> x6, matrix products: 93.4 us -> 13.5 us  [product(): jnp.einsum(spec, left, right, precision=HIGHEST, preferred_element_type=F32)]
    ppermute x18 -> x0, waiting for transfers between devices: 34.9 us -> none  [swapped(): return lax.ppermute(block, axis, route)]
    ppermute x18 -> x0, starting transfers between devices: 34.7 us -> none  [swapped(): return lax.ppermute(block, axis, route)]
  transfers between devices with their start and end apart: 37 -> 8, of which waited for: 37 -> 6; matrix products, arithmetic and copies ran while one was open for 1% -> 2% of each run, Pallas kernels for 0% -> 0%
where the time goes in v1:
time: 769 us
  waiting for transfers between devices  607 us (79%)
  Pallas kernels  94.8 us (12%)
  blocking collectives  24.5 us (3%)
  between operations  19.1 us (2%)
  matrix products  13.5 us (2%)
    reduce_scatter x1, waiting for transfers between devices, shards(): cw = lax.psum_scatter(full, 'pcol', scatter_dimension=1, tiled=True)  201 us
    reduce_scatter x1, waiting for transfers between devices, shards(): mixed = lax.psum_scatter(mixed, 'pcol', scatter_dimension=0, tiled=True)  139 us
    psum x1, waiting for transfers between devices, shards(): piece = lax.psum(jnp.where(q == p // per_row, piece, 0.0), 'prow')  120 us
    pallas_call x1, Pallas kernels, run_waves(): pl.pallas_call(functools.partial(waves, np_, nq), out_shape=jax.ShapeDtyp...  94.8 us
    all_gather x1, waiting for transfers between devices, shards(): at = lax.all_gather(outer, 'pcol', axis=0, tiled=True)[bs:]  72.1 us
    all_gather x1, waiting for transfers between devices, shards(): basis = lax.all_gather(take(column_bases, l_at), 'pcol', axis=0, tiled=True)  39.1 us
    reduce_scatter x1, waiting for transfers between devices, shards(): lax.psum_scatter(outer, 'pcol', scatter_dimension=0, axis_index_groups=bl...  35.5 us
    all_gather x1, blocking collectives, shards(): mixed = lax.all_gather(mixed, 'prow', axis=0)  24.5 us
  transfers between devices with their start and end apart: 8, of which 6 were waited for; matrix products, arithmetic and copies ran while one was open for 2% of the time, Pallas kernels for 0%

profile of v1, /device:TPU:1, one launch (start us, length us, event | category | flops | bytes accessed | tf_op | source)
XLA Modules:
  0.0 768.5 jit_solution(1472251251707352489)
XLA Ops:
  7.5 1.7 dynamic-slice_select_fusion
  9.2 1.9 fusion.14
  11.2 119.6 %all-reduce.3.cloned.1.call-done = f32[64,512]{1,0:T(8,128)} async-done(((f32[64,512]{1,0:T(8,128)}), f32[64,512]{1,0:T(8,128)}) %all-reduce.3.cloned.1.call-update) | async-done | bytes 131088 | tf_op jit(solution)/shard_map/psum | solution.py:197
  130.8 2.2 fusion.15
  133.1 0.6 dynamic_slice.32
  135.4 0.6 slice_bitcast_fusion
  136.1 1.0 fusion.2
  137.2 35.5 %reduce-scatter.12.cloned.1.call-done = f32[64,128]{1,0:T(8,128)} async-done(((f32[512,128]{1,0:T(8,128)}), f32[64,128]{1,0:T(8,128)}) %reduce-scatter.12.cloned.1.call-update) | async-done | bytes 32784 | tf_op jit(solution)/shard_map/reduce_scatter | solution.py:199
  172.8 0.6 dynamic_slice.30
  175.7 39.1 %all-gather.7.cloned.1.call-done = f32[1,512,512]{2,1,0:T(8,128)} async-done(((f32[1,16,512]{2,1,0:T(8,128)}), f32[1,512,512]{2,1,0:T(8,128)}) %all-gather.7.cloned.1.call-update) | async-done | bytes 1048592 | tf_op jit(solution)/shard_map/all_gather | solution.py:206
  214.8 1.8 fusion
  216.6 2.0 fusion.7
  218.8 0.8 dynamic-slice_bitcast_fusion
  219.6 0.8 constant_dynamic-slice_fusion
  220.3 4.6 convolution_bitcast_fusion
  224.9 0.7 broadcast_add_fusion.den
  225.7 72.1 %all-gather.5.cloned.1.call-done = f32[2048,128]{1,0:T(8,128)} async-done(((f32[64,128]{1,0:T(8,128)}), f32[2048,128]{1,0:T(8,128)}) %all-gather.5.cloned.1.call-update) | async-done | bytes 1048592 | tf_op jit(solution)/shard_map/all_gather | solution.py:200
  297.7 2.1 slice.104.at
  299.8 139.3 %reduce-scatter.14.cloned.1.call-done = f32[16,512]{1,0:T(8,128)} async-done(((f32[512,512]{1,0:T(8,128)}), f32[16,512]{1,0:T(8,128)}) %reduce-scatter.14.cloned.1.call-update) | async-done | bytes 32784 | tf_op jit(solution)/shard_map/reduce_scatter | solution.py:210
  439.1 24.5 %all-gather.1 = f32[256,512]{1,0:T(8,128)S(1)} all-gather(f32[16,512]{1,0:T(8,128)} %reduce-scatter.14.cloned.1.call-done), channel_id=3, replica_groups=mesh['prow'=16,'pcol'=32] {'prow'}, dimensions={0}, use_global_device_ids=true | all-gather | bytes 557056 | tf_op jit(solution)/shard_map/all_gather | solution.py:211
  463.8 0.1 fusion.4
  464.0 201.1 %reduce-scatter.8.cloned.1.call-done.cw = f32[6,16,128]{2,1,0:T(8,128)} async-done(((f32[6,512,128]{2,1,0:T(8,128)}), f32[6,16,128]{2,1,0:T(8,128)}) %reduce-scatter.8.cloned.1.call-update) | async-done | bytes 49168 | tf_op jit(solution)/shard_map/reduce_scatter | solution.py:191
  665.0 94.8 %shard_map.91 = f32[6,16,128]{2,1,0:T(8,128)} custom-call(f32[6,16,128]{2,1,0:T(8,128)} %reduce-scatter.8.cloned.1.call-done.cw, f32[1536,128]{1,0:T(8,128)} %slice.104.at, f32[6,96,512]{2,1,0:T(8,128)} %copy-done.2, f32[6,16,128]{2,1,0:T(8,128)} %broadcast_add_fusion.den, f32[128,512]{1,0:T(8,128)} %bases.1), custom_call_target="tpu_custom_call" | custom-call | tf_op jit(solution)/shard_map/pallas_call | solution.py:149
  759.8 1.4 copy.32
  (48 shorter events, 0.7 us)
Async XLA Ops:
  7.4 207.4 %copy-start = (f32[6,16,3072]{2,1,0:T(8,128)S(1)}, f32[6,16,3072]{2,1,0:T(8,128)}, u32[]{:S(2)}) copy-start(f32[6,16,3072]{2,1,0:T(8,128)} %param.15) | copy-start | bytes 3538948
  7.4 125.7 %copy-start.6 = (s32[16]{0:T(128)S(1)}, s32[16]{0:T(128)}, u32[]{:S(2)}) copy-start(s32[16]{0:T(128)} %constant.102.clone) | copy-start | bytes 196
  7.4 128.7 %copy-start.1 = (f32[128,512]{1,0:T(8,128)S(1)}, f32[128,512]{1,0:T(8,128)}, u32[]{:S(2)}) copy-start(f32[128,512]{1,0:T(8,128)} %bases.1) | copy-start | bytes 786436
  7.4 128.0 %copy-start.3 = (f32[6,16,512]{2,1,0:T(8,128)S(1)}, f32[6,16,512]{2,1,0:T(8,128)}, u32[]{:S(2)}) copy-start(f32[6,16,512]{2,1,0:T(8,128)} %param.13) | copy-start | bytes 589828
  7.4 128.7 %copy-start.4 = (f32[6,16,128]{2,1,0:T(8,128)S(1)}, f32[6,16,128]{2,1,0:T(8,128)}, u32[]{:S(2)}) copy-start(f32[6,16,128]{2,1,0:T(8,128)} %param.9) | copy-start | bytes 147460
  7.4 123.4 %all-reduce.3.cloned.1.call-start = ((), (), s32[]{:S(2)}) async-start(), calls=%async_computation.7 | async-start | bytes 262144 | tf_op jit(solution)/shard_map/psum | solution.py:197
  9.2 163.6 %copy-start.5 = (s32[16]{0:T(128)S(1)}, s32[16]{0:T(128)}, u32[]{:S(2)}) copy-start(s32[16]{0:T(128)} %constant.103.clone) | copy-start | bytes 196
  9.2 121.6 %reduce-scatter.10.cloned.1.call-start = ((), (), s32[]{:S(2)}) async-start(), calls=%async_computation.8 | async-start | bytes 163840 | tf_op jit(solution)/shard_map/reduce_scatter | solution.py:194
  11.1 161.6 %reduce-scatter.12.cloned.1.call-start = ((), (), s32[]{:S(2)}) async-start(), calls=%async_computation.9 | async-start | bytes 294912 | tf_op jit(solution)/shard_map/reduce_scatter | solution.py:199
  133.0 81.8 %all-gather.7.cloned.1.call-start = ((), (), s32[]{:S(2)}) async-start(), calls=%async_computation.12 | async-start | bytes 1081344 | tf_op jit(solution)/shard_map/all_gather | solution.py:206
  136.0 84.3 %reduce-scatter.6.cloned.1.call-start = ((), (), s32[]{:S(2)}) async-start(), calls=%async_computation.5 | async-start | bytes 245760 | tf_op jit(solution)/shard_map/reduce_scatter | solution.py:189
  137.1 160.6 %all-gather.5.cloned.1.call-start = ((), (), s32[]{:S(2)}) async-start(), calls=%async_computation.10 | async-start | bytes 1081344 | tf_op jit(solution)/shard_map/all_gather | solution.py:200
  172.7 266.4 %reduce-scatter.14.cloned.1.call-start = ((), (), s32[]{:S(2)}) async-start(), calls=%async_computation.11 | async-start | bytes 1081344 | tf_op jit(solution)/shard_map/reduce_scatter | solution.py:210
  218.6 446.4 %reduce-scatter.8.cloned.1.call-start = ((), (), s32[]{:S(2)}) async-start(), calls=%async_computation.6 | async-start | bytes 1622016 | tf_op jit(solution)/shard_map/reduce_scatter | solution.py:191
  463.9 201.1 %copy-start.2 = (f32[6,96,512]{2,1,0:T(8,128)}, f32[6,96,512]{2,1,0:T(8,128)S(1)}, u32[]{:S(2)}) copy-start(f32[6,96,512]{2,1,0:T(8,128)S(1)} %bitcast_dynamic-update-slice_fusion.lhs) | copy-start | bytes 3538948
Sparse Core Ops, SparseCore 0:
  10.5 120.2 all-reduce.2
  133.5 39.1 reduce-scatter.11
  175.5 27.1 reduce-scatter.5
  218.8 220.3 reduce-scatter.13
  443.4 221.5 reduce-scatter.7
Sparse Core Ops, SparseCore 1:
  12.5 28.4 reduce-scatter.9
  136.7 78.1 all-gather.6
  217.8 79.9 all-gather.4

commit v2 on v1

v2 whole, which is shorter than its diff:
```python
import functools

import jax
import jax.numpy as jnp
from jax import lax
from jax.experimental import pallas as pl
from jax.experimental.pallas import tpu as pltpu
from jax.sharding import PartitionSpec as P

RB = 4
CB = 6
PAIRS = CB * (CB - 1) // 2
MESH = pl.DeviceIdType.MESH
F32 = jnp.float32
BF16 = jnp.bfloat16
ROW_BY_COL = ((1,), (0,))
COL_BY_COL = ((0,), (0,))
ROW_BY_ROW = ((1,), (1,))


def halves(value):
    high = value.astype(BF16)
    low = (value - high.astype(F32)).astype(BF16)
    return high, low


def dot_of(left, right, dims):
    return lax.dot_general(left, right, (dims, ((), ())), preferred_element_type=F32)


def dot_split(left, right, dims):
    (left_high, left_low), (right_high, right_low) = left, right
    small = dot_of(left_low, right_high, dims) + dot_of(left_high, right_low, dims)
    return dot_of(left_high, right_high, dims) + small


def dot3(left, right, dims=ROW_BY_COL):
    return dot_split(halves(left), halves(right), dims)


def kernel(np_, nq, *refs):
    (rhs, coupling, bases, den, colbases, colcoup, out, *rest) = refs
    (upart, urecv, vpart, crecv, hpart, hrecv, pk, gpart, grecv, apiece, at) = rest[:11]
    (bx, qx, ql, tpart, trecv, tpiece, lhs) = rest[11:18]
    (yown, wown, yrow, ycol, wbuf, pend, acc, sems) = rest[18:]
    fw, ew = rhs.shape[1], rhs.shape[2]
    cww = coupling.shape[1]
    bs = fw * np_
    ns = nq // RB
    nx = bs // ew
    nz = np_ // nx
    zw = bs // nz
    nw = bs // cww
    per_row = ew // cww
    q = lax.axis_index("prow")
    p = lax.axis_index("pcol")
    i, s = q // ns, q % ns
    z, x = p // nx, p % nx
    k_own, w_own = p // nw, p % nw
    j_own = 1
    for first in range(2, CB):
        j_own = j_own + (q >= first * (first - 1) // 2).astype(jnp.int32)
    l_own = q - j_own * (j_own - 1) // 2
    has_pair = q < PAIRS
    has_coupling = k_own > i

    used = [0]

    def new_sem(count=1):
        at_sem = used[0]
        used[0] += count
        return [sems.at[at_sem + n] for n in range(count)]

    row_send, row_recv, col_send = new_sem(CB), new_sem(CB), new_sem(CB)
    col_recv = [new_sem(CB) for _ in range(RB - 1)]
    w_send, w_recv = new_sem(CB), new_sem(CB)
    c1_send, c1_recv, c2_send, c2_recv = new_sem(2), new_sem(2), new_sem(CB), new_sem(CB)
    (a1_send, a1_recv, a2_send, a2_recv, a3_send, a3_recv, a4_send) = new_sem(7)
    a4_recv = new_sem(RB - 1)
    (b1_send, b1_recv, q1_send, q1_recv, l1_send, l1_recv) = new_sem(6)
    (b2_send, b2_recv, b3_send) = new_sem(3)
    b3_recv = new_sem(CB - 1)

    def send(src, dst, send_sem, recv_sem, q_to, p_to):
        pltpu.make_async_remote_copy(
            src_ref=src,
            dst_ref=dst,
            send_sem=send_sem,
            recv_sem=recv_sem,
            device_id=(q_to, p_to),
            device_id_type=MESH,
        ).start()

    def keep(src, dst, recv_sem):
        pltpu.make_async_copy(src, dst, recv_sem).start()

    def wait(ref, sem):
        pltpu.make_async_copy(ref, ref, sem).wait()

    def rows_of(n, size):
        return pl.ds(pl.multiple_of(n * size, size), size)

    barrier = pltpu.get_barrier_semaphore()

    @pl.loop(1, np_)
    def _(d):
        pl.semaphore_signal(barrier, inc=1, device_id=(q, (p + d) % np_), device_id_type=MESH)

    @pl.loop(0, nq * nx)
    def _(t):
        q_to = t // nx

        @pl.when(q_to != q)
        def _():
            pl.semaphore_signal(
                barrier, inc=1, device_id=(q_to, z * nx + t % nx), device_id_type=MESH
            )

    bases_split = halves(bases[...])
    stacked = rhs[...].reshape(CB * fw, ew)
    first = dot_split(halves(stacked), bases_split, ROW_BY_COL)
    inner = dot_split(halves(coupling[...]), bases_split, COL_BY_COL)
    for n in range(ns):
        upart[n] = first[:, n * ew : (n + 1) * ew]
        hpart[n] = inner[:, n * ew : (n + 1) * ew]
    for l in range(CB):
        lhs[l, :fw] = colbases[l]

    pl.semaphore_wait(barrier, np_ - 1 + (nq - 1) * nx)

    chunks = (pl.ds(0, fw), pl.ds(fw, (CB - 1) * fw))

    def send_c1(c):
        @pl.loop(0, ns)
        def _(t):
            src, dst = upart.at[t, chunks[c]], urecv.at[s, chunks[c]]

            @pl.when(t == s)
            def _():
                keep(src, dst, c1_recv[c])

            @pl.when(t != s)
            def _():
                send(src, dst, c1_send[c], c1_recv[c], i * ns + t, p)

    send_c1(0)

    @pl.when(has_pair)
    def _():
        @pl.loop(0, np_)
        def _(t):
            src = colbases.at[l_own, :, rows_of(t % nx, ew)]
            dst = ql.at[rows_of(p, fw)]

            @pl.when(t == p)
            def _():
                keep(src, dst, l1_recv)

            @pl.when(t != p)
            def _():
                send(src, dst, l1_send, l1_recv, q, t)

        @pl.loop(0, nx)
        def _(t):
            src_b = colcoup.at[j_own, :, rows_of(l_own, bs)]
            src_q = colbases.at[j_own]
            dst_b, dst_q = bx.at[rows_of(x, fw)], qx.at[rows_of(x, fw)]

            @pl.when(t == x)
            def _():
                keep(src_b, dst_b, b1_recv)
                keep(src_q, dst_q, q1_recv)

            @pl.when(t != x)
            def _():
                send(src_b, dst_b, b1_send, b1_recv, q, z * nx + t)
                send(src_q, dst_q, q1_send, q1_recv, q, z * nx + t)

    @pl.when(has_coupling)
    def _():
        @pl.loop(0, ns)
        def _(t):
            @pl.when(t == s)
            def _():
                keep(hpart.at[t], hrecv.at[s], a1_recv)

            @pl.when(t != s)
            def _():
                send(hpart.at[t], hrecv.at[s], a1_send, a1_recv, i * ns + t, p)

    @pl.when(q == p // per_row)
    def _():
        @pl.loop(0, i * ns)
        def _(t):
            send(
                bases.at[rows_of(p % per_row, cww)],
                pk,
                a2_send,
                a2_recv,
                i * ns - 1 - t,
                p,
            )

    send_c1(1)

    def send_c2(j):
        @pl.loop(0, np_)
        def _(t):
            src, dst = vpart.at[j, rows_of(t, fw)], crecv.at[j, p]

            @pl.when(t == p)
            def _():
                keep(src, dst, c2_recv[j])

            @pl.when(t != p)
            def _():
                send(src, dst, c2_send[j], c2_recv[j], q, t)

    wait(urecv.at[:, chunks[0]], c1_recv[0])
    vpart[0] = dot3(colbases[0], jnp.sum(urecv[:, :fw], axis=0), COL_BY_COL)
    send_c2(0)

    @pl.when(has_pair)
    def _():
        wait(ql, l1_recv)
        wait(bx, b1_recv)
        wait(qx, q1_recv)
        mixed = dot3(bx[...], ql[...])
        tpart[...] = dot3(qx[...], mixed, COL_BY_COL)

        @pl.loop(0, nz)
        def _(t):
            src, dst = tpart.at[rows_of(t, zw)], trecv.at[z]

            @pl.when(t == z)
            def _():
                keep(src, dst, b2_recv)

            @pl.when(t != z)
            def _():
                send(src, dst, b2_send, b2_recv, q, t * nx + x)

    @pl.when(has_coupling)
    def _():
        wait(hrecv, a1_recv)
        wait(pk, a2_recv)
        gpart[...] = dot3(pk[...], jnp.sum(hrecv[...], axis=0), COL_BY_COL)

        @pl.loop(0, nw)
        def _(t):
            src, dst = gpart.at[rows_of(t, cww)], grecv.at[w_own]

            @pl.when(t == w_own)
            def _():
                keep(src, dst, a3_recv)

            @pl.when(t != w_own)
            def _():
                send(src, dst, a3_send, a3_recv, q, k_own * nw + t)

    wait(urecv.at[:, chunks[1]], c1_recv[1])
    for j in range(1, CB):
        left = jnp.sum(urecv[:, j * fw : (j + 1) * fw], axis=0)
        vpart[j] = dot3(colbases[j], left, COL_BY_COL)
    send_c2(1)

    own_rows = rows_of(p, fw)
    own_lanes = rows_of(s, ew)

    def sum_up(j):
        wait(crecv.at[j], c2_recv[j])
        pend[j] += jnp.sum(crecv[j], axis=0)

    def finish(j):
        yown[j] = acc[...] / den[j]
        yrow[j, own_rows, :] = yown[j]

        @pl.loop(1, np_)
        def _(d):
            send(
                yown.at[j],
                yrow.at[j, own_rows],
                row_send[j],
                row_recv[j],
                q,
                (p + d) % np_,
            )

        for k in range(1, RB):

            @pl.when(i == k)
            def _(k=k):
                @pl.loop(0, k * ns)
                def _(t):
                    send(
                        yown.at[j],
                        ycol.at[k - 1, j, :, own_lanes],
                        col_send[j],
                        col_recv[k - 1][j],
                        k * ns - 1 - t,
                        p,
                    )

    def left_terms(j):
        for k in range(1, RB):

            @pl.when(k > i)
            def _(k=k):
                if j == 0:
                    wait(at.at[k * bs : (k + 1) * bs], a4_recv[k - 1])
                wait(ycol.at[k - 1, j], col_recv[k - 1][j])
                acc[...] -= dot3(ycol[k - 1, j], at[k * bs : (k + 1) * bs])

    pend[...] = jnp.zeros_like(pend)
    sum_up(0)
    acc[...] = pend[0]

    @pl.when(i == RB - 1)
    def _():
        finish(0)

    @pl.when(has_pair)
    def _():
        wait(trecv, b2_recv)
        tpiece[...] = jnp.sum(trecv[...], axis=0)

        for l in range(CB - 1):

            @pl.when(l_own == l)
            def _(l=l):
                @pl.loop(0, nq * nx)
                def _(t):
                    q_to, x_to = t // nx, t % nx
                    src = tpiece.at[rows_of(x_to, fw)]
                    dst = lhs.at[l, rows_of(j_own - l, fw), rows_of(x, ew)]
                    here = jnp.logical_and(q_to == q, x_to == x)

                    @pl.when(here)
                    def _():
                        keep(src, dst, b3_recv[l])

                    @pl.when(jnp.logical_not(here))
                    def _():
                        send(src, dst, b3_send, b3_recv[l], q_to, z * nx + x_to)

    @pl.when(has_coupling)
    def _():
        wait(grecv, a3_recv)
        apiece[...] = jnp.sum(grecv[...], axis=0)
        for k in range(1, RB):

            @pl.when(k_own == k)
            def _(k=k):
                @pl.loop(0, np_)
                def _(t):
                    dst = at.at[rows_of(p, cww)]

                    @pl.when(t == p)
                    def _():
                        keep(apiece, dst, a4_recv[k - 1])

                    @pl.when(t != p)
                    def _():
                        send(apiece, dst, a4_send, a4_recv[k - 1], q, t)

    for j in range(CB):
        if j == 0:

            @pl.when(i < RB - 1)
            def _():
                left_terms(0)
                finish(0)

        else:
            sum_up(j)
            acc[...] = pend[j]
            left_terms(j)
            finish(j)
        if j + 2 < CB:
            send_c2(j + 2)

        wait(yrow.at[j, pl.ds(0, bs - fw)], row_recv[j])
        if j < CB - 1:
            wait(lhs.at[j, fw : (CB - j) * fw], b3_recv[j])
        both = dot3(lhs[j, : (CB - j) * fw], yrow[j])
        wown[j] = both[:fw]
        for later in range(j + 1, CB):
            at_row = (later - j) * fw
            pend[later] -= both[at_row : at_row + fw]
        wbuf[j, :, own_lanes] = wown[j]

        @pl.loop(1, ns)
        def _(d):
            send(
                wown.at[j],
                wbuf.at[j, :, own_lanes],
                w_send[j],
                w_recv[j],
                i * ns + (s + d) % ns,
                p,
            )

    for j in range(CB):
        wait(wbuf.at[j, :, pl.ds(0, (ns - 1) * ew)], w_recv[j])
        out[j] = dot_split(halves(wbuf[j]), halves(bases[...]), ROW_BY_ROW)

    for c in range(2):
        wait(urecv.at[pl.ds(0, ns - 1), chunks[c]], c1_send[c])
    for j in range(CB):
        wait(crecv.at[j, pl.ds(0, np_ - 1)], c2_send[j])
        wait(yrow.at[j, pl.ds(0, bs - fw)], row_send[j])
        wait(wbuf.at[j, :, pl.ds(0, (ns - 1) * ew)], w_send[j])
        for k in range(1, RB):

            @pl.when(i == k)
            def _(k=k):
                wait(yrow.at[j, pl.ds(0, fw * k * ns)], col_send[j])

    @pl.when(has_coupling)
    def _():
        wait(hrecv.at[pl.ds(0, ns - 1)], a1_send)
        wait(grecv.at[pl.ds(0, nw - 1)], a3_send)
        wait(at.at[pl.ds(0, (np_ - 1) * cww)], a4_send)

    for k in range(1, RB):

        @pl.when(jnp.logical_and(i == k, q == p // per_row))
        def _(k=k):
            wait(yrow.at[pl.ds(0, k * ns * cww // ew)], a2_send)

    @pl.when(has_pair)
    def _():
        wait(bx.at[pl.ds(0, (nx - 1) * fw)], b1_send)
        wait(qx.at[pl.ds(0, (nx - 1) * fw)], q1_send)
        wait(ql.at[pl.ds(0, bs - fw)], l1_send)
        wait(trecv.at[pl.ds(0, nz - 1)], b2_send)
        wait(at.at[pl.ds(0, (nq * nx - 1) * fw)], b3_send)


def shards(np_, nq, right_side, coupling, row_bases, row_values, column_bases, column_values, column_coupling):
    ns = nq // RB
    fw, ew = right_side.shape[1], right_side.shape[2]
    cww = coupling.shape[1]
    bs = row_bases.shape[1]
    nx = bs // ew
    nz = np_ // nx
    zw = bs // nz
    nw = bs // cww
    q = lax.axis_index("prow")
    p = lax.axis_index("pcol")
    i, s = q // ns, q % ns
    own_values = lax.dynamic_slice(row_values, (i, s * ew), (1, ew))
    own_shifts = lax.dynamic_slice_in_dim(column_values, p * fw, fw, 1)
    den = own_shifts[:, :, None] + own_values[:, None, :]
    vmem = pl.BlockSpec(memory_space=pltpu.VMEM)
    scratch = (
        (ns, CB * fw, ew),
        (ns, CB * fw, ew),
        (CB, bs, ew),
        (CB, np_, fw, ew),
        (ns, cww, ew),
        (ns, cww, ew),
        (cww, bs),
        (bs, ew),
        (nw, cww, ew),
        (cww, ew),
        (RB * bs, ew),
        (nx * fw, bs),
        (nx * fw, bs),
        (bs, ew),
        (bs, ew),
        (nz, zw, ew),
        (zw, ew),
        (CB, CB * fw, bs),
        (CB, fw, ew),
        (CB, fw, ew),
        (CB, bs, ew),
        (RB - 1, CB, fw, bs),
        (CB, fw, bs),
        (CB, fw, ew),
        (fw, ew),
    )
    return pl.pallas_call(
        functools.partial(kernel, np_, nq),
        out_shape=jax.ShapeDtypeStruct((CB, fw, ew), F32),
        in_specs=[vmem] * 6,
        out_specs=vmem,
        scratch_shapes=[pltpu.VMEM(shape, F32) for shape in scratch]
        + [pltpu.SemaphoreType.DMA((96,))],
        compiler_params=pltpu.CompilerParams(collective_id=0, has_side_effects=True),
    )(right_side, coupling, row_bases, den, column_bases, column_coupling)


def solution(mesh):
    placed = (
        P(None, "pcol", "prow"),
        P("prow", "pcol"),
        P("prow", None),
        P(),
        P(None, "pcol", None),
        P(),
        P(None, "pcol", None),
    )
    body = functools.partial(shards, mesh.shape["pcol"], mesh.shape["prow"])
    return jax.shard_map(
        body, mesh=mesh, in_specs=placed, out_specs=P(None, "pcol", "prow"), check_vma=False
    )
```

time: 769 us -> 153 us (0.20)
  waiting for transfers between devices: 607 us -> 0 us
  Pallas kernels: 94.8 us -> 149 us
  blocking collectives: 24.5 us -> 0 us
  between operations: 19.1 us -> 0.01 us
  matrix products: 13.5 us -> 0 us
    reduce_scatter x5 -> x0, waiting for transfers between devices: 376 us -> none  [the longest x1 201 us: shards(): cw = lax.psum_scatter(full, 'pcol', scatter_dimension=1, tiled=True)]
    psum x1 -> x0, waiting for transfers between devices: 120 us -> none  [shards(): piece = lax.psum(jnp.where(q == p // per_row, piece, 0.0), 'prow')]
    all_gather x2 -> x0, waiting for transfers between devices: 111 us -> none  [the longest x1 72.1 us: shards(): at = lax.all_gather(outer, 'pcol', axis=0, tiled=True)[bs:]]
    pallas_call x1, Pallas kernels: 94.8 us -> 149 us  [shards(): pl.pallas_call(functools.partial(kernel, np_, nq), out_shape=jax.ShapeDty...]
    all_gather x1 -> x0, blocking collectives: 24.5 us -> none  [shards(): mixed = lax.all_gather(mixed, 'prow', axis=0)]
    dot_general x6 -> x0, matrix products: 13.5 us -> none  [product(): jnp.einsum(spec, left, right, precision=HIGHEST, preferred_element_type=F32)]
  transfers between devices with their start and end apart: 8 -> 0, of which waited for: 6 -> 0; matrix products, arithmetic and copies ran while one was open for 2% -> 0% of each run, Pallas kernels for 0% -> 0%
where the time goes in v2:
time: 153 us
  Pallas kernels  149 us (97%)
  local copies, waits for them, and re-layouts  3.74 us (2%)
    pallas_call x1, Pallas kernels, shards(): pl.pallas_call(functools.partial(kernel, np_, nq), out_shape=jax.ShapeDty...  149 us

profile of v2, /device:TPU:1, one launch (start us, length us, event | category | flops | bytes accessed | tf_op | source)
XLA Modules:
  0.0 153.2 jit_solution(12761941839231051427)
XLA Ops:
  0.0 0.0 copy-start
  0.0 0.8 dynamic-slice_bitcast_fusion
  0.8 0.0 copy-done
  0.8 0.1 constant_dynamic-slice_fusion
  0.8 0.7 broadcast_add_fusion.refs_3_
  1.6 1.5 copy.8.refs_1_
  3.0 148.7 %shard_map.73 = f32[6,16,128]{2,1,0:T(8,128)} custom-call(f32[6,16,128]{2,1,0:T(8,128)} %refs_0_.1, f32[128,64]{1,0:T(8,128)} %copy.8.refs_1_, f32[128,512]{1,0:T(8,128)} %refs_2_.1, f32[6,16,128]{2,1,0:T(8,128)} %broadcast_add_fusion.refs_3_, f32[6,16,512]{2,1,0:T(8,128)} %refs_4_.1, f32[6,16,3072]{2,1,0:T(8,128)} %refs_5_.1), custom_call_target="tpu_custom_call" | custom-call | tf_op jit(solution)/shard_map/pallas_call | solution.py:483
  151.7 1.4 copy.10
Async XLA Ops:
  0.0 0.8 copy-start

commit v3 on v2

v3 whole, which is shorter than its diff:
```python
import functools

import jax
import jax.numpy as jnp
from jax import lax
from jax.experimental import pallas as pl
from jax.experimental.pallas import tpu as pltpu
from jax.sharding import PartitionSpec as P

RB = 4
CB = 6
PAIRS = CB * (CB - 1) // 2
MESH = pl.DeviceIdType.MESH
F32 = jnp.float32
BF16 = jnp.bfloat16
ROW_BY_COL = ((1,), (0,))
COL_BY_COL = ((0,), (0,))
ROW_BY_ROW = ((1,), (1,))


def halves(value):
    high = value.astype(BF16)
    low = (value - high.astype(F32)).astype(BF16)
    return high, low


def dot_of(left, right, dims):
    return lax.dot_general(left, right, (dims, ((), ())), preferred_element_type=F32)


def dot_split(left, right, dims):
    (left_high, left_low), (right_high, right_low) = left, right
    small = dot_of(left_low, right_high, dims) + dot_of(left_high, right_low, dims)
    return dot_of(left_high, right_high, dims) + small


def dot3(left, right, dims=ROW_BY_COL):
    return dot_split(halves(left), halves(right), dims)


def kernel(np_, nq, *refs):
    (rhs, coupling, bases, row_values, colbases, col_values, colcoup, out, *rest) = refs
    (upart, urecv, ux, uown, qside, vpart, crecv) = rest[:7]
    (hpart, hrecv, pk, gpart, grecv, apiece, at) = rest[7:14]
    (bx, qx, ql, tpart, trecv, tpiece, lhs) = rest[14:21]
    (yown, wown, yrow, ycol, wbuf, pend, den, acc, sems) = rest[21:]
    fw, ew = rhs.shape[1], rhs.shape[2]
    cww = coupling.shape[0]
    bs = fw * np_
    ns = nq // RB
    nx = bs // ew
    nz = np_ // nx
    nw = bs // cww
    per_row = ew // cww
    q = lax.axis_index("prow")
    p = lax.axis_index("pcol")
    i, s = q // ns, q % ns
    z, x = p // nx, p % nx
    k_own, w_own = p // nw, p % nw
    pair = nq - 1 - q
    j_own = 1
    for first in range(2, CB):
        j_own = j_own + (pair >= first * (first - 1) // 2).astype(jnp.int32)
    l_own = pair - j_own * (j_own - 1) // 2
    has_pair = pair < PAIRS
    has_coupling = k_own > i

    used = [0]

    def new_sem(count=1):
        at_sem = used[0]
        used[0] += count
        return [sems.at[at_sem + n] for n in range(count)]

    row_send, row_recv, col_send = new_sem(CB), new_sem(CB), new_sem(CB)
    col_recv = [new_sem(CB) for _ in range(RB - 1)]
    w_send, w_recv = new_sem(CB), new_sem(CB)
    c1_send, c1_recv, c2_send, c2_recv = new_sem(2), new_sem(2), new_sem(2), new_sem(2)
    c3_send, c3_recv, q2_send, q2_recv = new_sem(2), new_sem(2), new_sem(2), new_sem(2)
    a1_send, a1_recv, a2_send, a2_recv, a2_pass, a3_send = new_sem(6)
    a3_recv, a4_send, a4_recv = new_sem(RB - 1), new_sem(RB - 1), new_sem(RB - 1)
    b1_send, b1_recv, q1_send, q1_recv, l1_send, l1_recv = new_sem(6)
    b2_send, b2_recv, b3_send = new_sem(3)
    b3_recv = new_sem(CB - 1)

    def send(src, dst, send_sem, recv_sem, q_to, p_to):
        pltpu.make_async_remote_copy(
            src_ref=src,
            dst_ref=dst,
            send_sem=send_sem,
            recv_sem=recv_sem,
            device_id=(q_to, p_to),
            device_id_type=MESH,
        ).start()

    def send_or_keep(here, src, dst, send_sem, recv_sem, q_to, p_to):
        @pl.when(here)
        def _():
            pltpu.make_async_copy(src, dst, recv_sem).start()

        @pl.when(jnp.logical_not(here))
        def _():
            send(src, dst, send_sem, recv_sem, q_to, p_to)

    def wait(ref, sem, name="w"):
        pltpu.make_async_copy(ref, ref, sem).wait()

    def rows_of(n, size):
        return pl.ds(pl.multiple_of(n * size, size), size)

    def far_first(d):
        return (p + (d + np_ // 2 - 1) % (np_ - 1) + 1) % np_

    barrier = pltpu.get_barrier_semaphore()

    @pl.loop(0, np_ - 1)
    def _(d):
        pl.semaphore_signal(barrier, inc=1, device_id=(q, far_first(d)), device_id_type=MESH)

    @pl.loop(1, nq)
    def _(d):
        for x_to in range(nx):
            pl.semaphore_signal(
                barrier, inc=1, device_id=((q + d) % nq, z * nx + x_to), device_id_type=MESH
            )

    bases_split = halves(bases[...])
    stacked = rhs[...].reshape(CB * fw, ew)
    first = dot_split(halves(stacked), bases_split, ROW_BY_COL)
    inner = dot_split(halves(coupling[...]), bases_split, ROW_BY_COL)
    for n in range(ns):
        upart[n] = first[:, n * ew : (n + 1) * ew]
        hpart[n] = inner[:, n * ew : (n + 1) * ew]
    for l in range(CB):
        lhs[l, :fw] = colbases[l]
    own_lanes = rows_of(s, ew)
    values = row_values[:, own_lanes]
    own_value = lax.broadcasted_iota(jnp.int32, values.shape, 0) == i
    eigen = jnp.sum(jnp.where(own_value, values, 0.0), axis=0, keepdims=True)
    lanes = lax.broadcasted_iota(jnp.int32, (fw, ew), 1)
    chosen = lanes == z * fw + lax.broadcasted_iota(jnp.int32, (fw, ew), 0)
    for j in range(CB):
        shifts = col_values[pl.ds(j, 1), rows_of(x, ew)]
        shift = jnp.sum(jnp.where(chosen, shifts, 0.0), axis=1, keepdims=True)
        den[j] = shift + eigen

    pl.semaphore_wait(barrier, np_ - 1 + (nq - 1) * nx)

    chunks = (pl.ds(0, fw), pl.ds(fw, (CB - 1) * fw))
    blocks = (pl.ds(0, 1), pl.ds(1, CB - 1))

    def send_c1(c):
        @pl.loop(0, ns)
        def _(t):
            src, dst = upart.at[t, chunks[c]], urecv.at[s, chunks[c]]
            send_or_keep(t == s, src, dst, c1_send[c], c1_recv[c], i * ns + t, p)

    def send_q2(c):
        @pl.loop(0, nx)
        def _(t):
            src, dst = colbases.at[blocks[c], :, rows_of(t, ew)], qside.at[blocks[c], x]
            send_or_keep(t == x, src, dst, q2_send[c], q2_recv[c], q, z * nx + t)

    def send_c2(c):
        wait(urecv.at[:, chunks[c]], c1_recv[c], "c1_%d" % c)
        count = (1, CB - 1)[c]
        summed = jnp.sum(urecv[:, chunks[c]], axis=0)
        uown[blocks[c]] = summed.reshape(count, fw, ew)

        @pl.loop(0, nx)
        def _(t):
            src, dst = uown.at[blocks[c]], ux.at[blocks[c], x]
            send_or_keep(t == x, src, dst, c2_send[c], c2_recv[c], q, z * nx + t)

    def send_c3(c):
        wait(ux.at[blocks[c]], c2_recv[c], "c2_%d" % c)
        wait(qside.at[blocks[c]], q2_recv[c], "q2_%d" % c)
        for j in ((0,), tuple(range(1, CB)))[c]:
            left = qside[j].reshape(nx * fw, ew)
            right = ux[j].reshape(nx * fw, ew)
            vpart[j] = dot3(left, right, COL_BY_COL).reshape(nz, fw, ew)

        @pl.loop(0, nz)
        def _(t):
            src, dst = vpart.at[blocks[c], t], crecv.at[blocks[c], z]
            send_or_keep(t == z, src, dst, c3_send[c], c3_recv[c], q, t * nx + x)

    send_c1(0)
    send_q2(0)

    @pl.when(has_pair)
    def _():
        @pl.loop(0, nx)
        def _(t):
            src_b = colcoup.at[j_own, :, rows_of(l_own, bs)]
            src_q = colbases.at[j_own]
            dst_b, dst_q = bx.at[rows_of(x, fw)], qx.at[rows_of(x, fw)]
            send_or_keep(t == x, src_b, dst_b, b1_send, b1_recv, q, z * nx + t)
            send_or_keep(t == x, src_q, dst_q, q1_send, q1_recv, q, z * nx + t)

        dst = ql.at[rows_of(p, fw)]
        own = colbases.at[l_own, :, rows_of(x, ew)]
        pltpu.make_async_copy(own, dst, l1_recv).start()

        @pl.loop(0, np_ - 1)
        def _(d):
            to = far_first(d)
            src = colbases.at[l_own, :, rows_of(to % nx, ew)]
            send(src, dst, l1_send, l1_recv, q, to)

    core = q % 2
    partner = q + 1 - 2 * core
    piece = bases.at[rows_of(p % per_row, cww)]
    holder = p // per_row

    @pl.when(has_coupling)
    def _():
        @pl.loop(0, ns)
        def _(t):
            send_or_keep(t == s, hpart.at[t], hrecv.at[s], a1_send, a1_recv, i * ns + t, p)

    @pl.when(q == holder)
    def _():
        @pl.loop(0, i * ns // 2)
        def _(t):
            send(piece, pk, a2_send, a2_recv, i * ns - 2 - 2 * t + core, p)

    send_c2(0)

    @pl.when(has_coupling)
    def _():
        wait(hrecv, a1_recv, "a1")
        wait(pk, a2_recv, "a2")

        @pl.when(core == holder % 2)
        def _():
            send(pk, pk, a2_pass, a2_recv, partner, p)

        gpart[...] = dot3(pk[...], jnp.sum(hrecv[...], axis=0), COL_BY_COL)
        for k in range(1, RB):

            @pl.when(k_own == k)
            def _(k=k):
                dst = grecv.at[k - 1, w_own]
                pltpu.make_async_copy(gpart.at[rows_of(p, fw)], dst, a3_recv[k - 1]).start()

                @pl.loop(0, np_ - 1)
                def _(d):
                    to = far_first(d)
                    send(gpart.at[rows_of(to, fw)], dst, a3_send, a3_recv[k - 1], q, to)

    @pl.when(has_pair)
    def _():
        wait(bx, b1_recv, "bx")
        wait(qx, q1_recv, "qx")
        wait(ql, l1_recv, "ql")
        mixed = dot3(bx[...], ql[...])
        tpart[...] = dot3(qx[...], mixed, COL_BY_COL).reshape(nx, nz, fw, ew)

        @pl.loop(0, nz)
        def _(t):
            src, dst = tpart.at[:, t], trecv.at[z]
            send_or_keep(t == z, src, dst, b2_send, b2_recv, q, t * nx + x)

    send_c3(0)

    for k in range(RB - 1, 0, -1):

        @pl.when(k > i)
        def _(k=k):
            wait(grecv.at[k - 1], a3_recv[k - 1], "a3_%d" % k)
            apiece[k - 1] = jnp.sum(grecv[k - 1], axis=0)
            dst = at.at[k, rows_of(p, fw)]
            pltpu.make_async_copy(apiece.at[k - 1], dst, a4_recv[k - 1]).start()

            @pl.loop(0, np_ - 1)
            def _(d):
                send(apiece.at[k - 1], dst, a4_send[k - 1], a4_recv[k - 1], q, far_first(d))

    own_rows = rows_of(x * nz + z, fw)

    def finish(j):
        yown[j] = acc[...] / den[j]
        for k in range(1, RB):

            @pl.when(i == k)
            def _(k=k):
                @pl.loop(0, k * ns)
                def _(t):
                    send(
                        yown.at[j],
                        ycol.at[k - 1, j, :, own_lanes],
                        col_send[j],
                        col_recv[k - 1][j],
                        k * ns - 1 - t,
                        p,
                    )

        @pl.loop(0, np_ - 1)
        def _(d):
            dst = yrow.at[j, own_rows]
            send(yown.at[j], dst, row_send[j], row_recv[j], q, far_first(d))

        yrow[j, own_rows, :] = yown[j]

    def left_terms(j):
        for k in range(RB - 1, 0, -1):

            @pl.when(k > i)
            def _(k=k):
                if j == 0:
                    wait(at.at[k], a4_recv[k - 1], "a4_%d" % k)
                wait(ycol.at[k - 1, j], col_recv[k - 1][j], "col_%d_%d" % (k, j))
                acc[...] -= dot3(ycol[k - 1, j], at[k])

    def last_product(j):
        wait(wbuf.at[j, :, pl.ds(0, (ns - 1) * ew)], w_recv[j], "wx_%d" % j)
        out[j] = dot3(wbuf[j], bases[...], ROW_BY_ROW)

    wait(crecv.at[blocks[0]], c3_recv[0], "c3_0")
    acc[...] = jnp.sum(crecv[0], axis=0)

    @pl.when(i == RB - 1)
    def _():
        finish(0)

    @pl.when(has_pair)
    def _():
        wait(trecv, b2_recv, "b2")
        tpiece[...] = jnp.sum(trecv[...], axis=0)

        for l in range(CB - 1):

            @pl.when(l_own == l)
            def _(l=l):
                @pl.loop(0, nq * nx)
                def _(t):
                    q_to, x_to = nq - 1 - t // nx, t % nx
                    dst = lhs.at[l, rows_of(j_own - l, fw), rows_of(x, ew)]
                    here = jnp.logical_and(q_to == q, x_to == x)
                    to = z * nx + x_to
                    send_or_keep(here, tpiece.at[x_to], dst, b3_send, b3_recv[l], q_to, to)

    send_c1(1)
    send_q2(1)

    @pl.when(i < RB - 1)
    def _():
        left_terms(0)
        finish(0)

    send_c2(1)
    send_c3(1)
    wait(crecv.at[blocks[1]], c3_recv[1], "c3_1")
    for j in range(1, CB):
        pend[j] = jnp.sum(crecv[j], axis=0)

    for j in range(CB):
        if j > 0:
            acc[...] = pend[j]
            left_terms(j)
            finish(j)
            last_product(j - 1)

        wait(yrow.at[j, pl.ds(0, bs - fw)], row_recv[j], "row_%d" % j)
        if j < CB - 1:
            wait(lhs.at[j, fw : (CB - j) * fw], b3_recv[j], "b3_%d" % j)
        both = dot3(lhs[j, : (CB - j) * fw], yrow[j])
        wown[j] = both[:fw]
        for later in range(j + 1, CB):
            at_row = (later - j) * fw
            pend[later] -= both[at_row : at_row + fw]
        wbuf[j, :, own_lanes] = wown[j]

        @pl.loop(1, ns)
        def _(d):
            send(
                wown.at[j],
                wbuf.at[j, :, own_lanes],
                w_send[j],
                w_recv[j],
                i * ns + (s + d) % ns,
                p,
            )

    last_product(CB - 1)

    for c in range(2):
        wait(urecv.at[pl.ds(0, ns - 1), chunks[c]], c1_send[c])
        wait(ux.at[blocks[c], pl.ds(0, nx - 1)], c2_send[c])
        wait(qside.at[blocks[c], pl.ds(0, nx - 1)], q2_send[c])
        wait(crecv.at[blocks[c], pl.ds(0, nz - 1)], c3_send[c])
    for j in range(CB):
        wait(yrow.at[j, pl.ds(0, bs - fw)], row_send[j])
        wait(wbuf.at[j, :, pl.ds(0, (ns - 1) * ew)], w_send[j])
        for k in range(1, RB):

            @pl.when(i == k)
            def _(k=k):
                wait(yrow.at[j, pl.ds(0, fw * k * ns)], col_send[j])

    for k in range(1, RB):

        @pl.when(k > i)
        def _(k=k):
            wait(at.at[k, pl.ds(0, bs - fw)], a4_send[k - 1])

        @pl.when(jnp.logical_and(i == k, q == holder))
        def _(k=k):
            wait(yrow.at[pl.ds(0, k * ns * cww // (2 * ew))], a2_send)

    @pl.when(has_coupling)
    def _():
        wait(hrecv.at[pl.ds(0, ns - 1)], a1_send)
        wait(gpart.at[pl.ds(0, bs - fw)], a3_send)

        @pl.when(core == holder % 2)
        def _():
            wait(pk, a2_pass)

    @pl.when(has_pair)
    def _():
        wait(bx.at[pl.ds(0, (nx - 1) * fw)], b1_send)
        wait(qx.at[pl.ds(0, (nx - 1) * fw)], q1_send)
        wait(ql.at[pl.ds(0, bs - fw)], l1_send)
        wait(trecv.at[pl.ds(0, nz - 1)], b2_send)
        wait(yrow.at[pl.ds(0, 2), pl.ds(0, (nq * nx - 1) * fw // 2)], b3_send)


def shards(np_, nq, right_side, coupling, row_bases, row_values, column_bases, column_values, column_coupling):
    ns = nq // RB
    fw, ew = right_side.shape[1], right_side.shape[2]
    cww = coupling.shape[1]
    bs = row_bases.shape[1]
    nx = bs // ew
    nz = np_ // nx
    nw = bs // cww
    vmem = pl.BlockSpec(memory_space=pltpu.VMEM)
    scratch = (
        (ns, CB * fw, ew),
        (ns, CB * fw, ew),
        (CB, nx, fw, ew),
        (CB, fw, ew),
        (CB, nx, fw, ew),
        (CB, nz, fw, ew),
        (CB, nz, fw, ew),
        (ns, cww, ew),
        (ns, cww, ew),
        (cww, bs),
        (bs, ew),
        (RB - 1, nw, fw, ew),
        (RB - 1, fw, ew),
        (RB, bs, ew),
        (nx * fw, bs),
        (nx * fw, bs),
        (bs, ew),
        (nx, nz, fw, ew),
        (nz, nx, fw, ew),
        (nx, fw, ew),
        (CB, CB * fw, bs),
        (CB, fw, ew),
        (CB, fw, ew),
        (CB, bs, ew),
        (RB - 1, CB, fw, bs),
        (CB, fw, bs),
        (CB, fw, ew),
        (CB, fw, ew),
        (fw, ew),
    )
    return pl.pallas_call(
        functools.partial(kernel, np_, nq),
        out_shape=jax.ShapeDtypeStruct((CB, fw, ew), F32),
        in_specs=[vmem] * 7,
        out_specs=vmem,
        scratch_shapes=[pltpu.VMEM(shape, F32) for shape in scratch]
        + [pltpu.SemaphoreType.DMA((96,))],
        compiler_params=pltpu.CompilerParams(collective_id=0, has_side_effects=True),
    )(
        right_side,
        coupling.T,
        row_bases,
        row_values,
        column_bases,
        column_values,
        column_coupling,
    )


def solution(mesh):
    placed = (
        P(None, "pcol", "prow"),
        P("prow", "pcol"),
        P("prow", None),
        P(),
        P(None, "pcol", None),
        P(),
        P(None, "pcol", None),
    )
    body = functools.partial(shards, mesh.shape["pcol"], mesh.shape["prow"])
    return jax.shard_map(
        body, mesh=mesh, in_specs=placed, out_specs=P(None, "pcol", "prow"), check_vma=False
    )
```

time: 153 us -> 140 us (0.915)
  Pallas kernels: 149 us -> 138 us
  local copies, waits for them, and re-layouts: 3.74 us -> 1.42 us
    pallas_call x1, Pallas kernels: 149 us -> 138 us  [shards(): pl.pallas_call(functools.partial(kernel, np_, nq), out_shape=jax.ShapeDty...]
where the time goes in v3:
time: 140 us
  Pallas kernels  138 us (99%)
  local copies, waits for them, and re-layouts  1.42 us (1%)
    pallas_call x1, Pallas kernels, shards(): pl.pallas_call(functools.partial(kernel, np_, nq), out_shape=jax.ShapeDty...  138 us

profile of v3, /device:TPU:1, one launch (start us, length us, event | category | flops | bytes accessed | tf_op | source)
XLA Modules:
  0.0 139.6 jit_solution(13529534154156971400)
XLA Ops:
  0.0 138.1 %shard_map.73 = f32[6,16,128]{2,1,0:T(8,128)} custom-call(f32[6,16,128]{2,1,0:T(8,128)} %refs_0_.1, f32[64,128]{1,0:T(8,128)} %bitcast.1, f32[128,512]{1,0:T(8,128)} %refs_2_.1, f32[4,512]{1,0:T(4,128)} %refs_3_.1, f32[6,16,512]{2,1,0:T(8,128)} %refs_4_.1, f32[6,512]{1,0:T(8,128)} %refs_5_.1, f32[6,16,3072]{2,1,0:T(8,128)} %refs_6_.1), custom_call_target="tpu_custom_call" | custom-call | tf_op jit(solution)/shard_map/pallas_call | solution.py:470
  138.2 1.4 %copy.9 = f32[6,16,128]{2,1,0:T(8,128)} copy(f32[6,16,128]{2,1,0:T(8,128)} %shard_map.73) | data formatting | bytes 98304

commit v4 on v3

--- a/solution.py
+++ b/solution.py
@@ -81,7 +81,9 @@
     a3_recv, a4_send, a4_recv = new_sem(RB - 1), new_sem(RB - 1), new_sem(RB - 1)
     b1_send, b1_recv, q1_send, q1_recv, l1_send, l1_recv = new_sem(6)
     b2_send, b2_recv, b3_send = new_sem(3)
-    b3_recv = new_sem(CB - 1)
+    b3_pass = new_sem(PAIRS)
+    b3_base = used[0]
+    b3_recv = new_sem(PAIRS)
 
     def send(src, dst, send_sem, recv_sem, q_to, p_to):
         pltpu.make_async_remote_copy(
@@ -131,8 +133,6 @@
     for n in range(ns):
         upart[n] = first[:, n * ew : (n + 1) * ew]
         hpart[n] = inner[:, n * ew : (n + 1) * ew]
-    for l in range(CB):
-        lhs[l, :fw] = colbases[l]
     own_lanes = rows_of(s, ew)
     values = row_values[:, own_lanes]
     own_value = lax.broadcasted_iota(jnp.int32, values.shape, 0) == i
@@ -185,11 +185,15 @@
             src, dst = vpart.at[blocks[c], t], crecv.at[blocks[c], z]
             send_or_keep(t == z, src, dst, c3_send[c], c3_recv[c], q, t * nx + x)
 
-    send_c1(0)
-    send_q2(0)
-
-    @pl.when(has_pair)
-    def _():
+    core = q % 2
+    partner = q + 1 - 2 * core
+    piece = bases.at[rows_of(p % per_row, cww)]
+    holder = p // per_row
+    top = i == RB - 1
+    early_pair = jnp.logical_and(has_pair, top)
+    late_pair = jnp.logical_and(has_pair, i < RB - 1)
+
+    def send_b1():
         @pl.loop(0, nx)
         def _(t):
             src_b = colcoup.at[j_own, :, rows_of(l_own, bs)]
@@ -208,49 +212,7 @@
             src = colbases.at[l_own, :, rows_of(to % nx, ew)]
             send(src, dst, l1_send, l1_recv, q, to)
 
-    core = q % 2
-    partner = q + 1 - 2 * core
-    piece = bases.at[rows_of(p % per_row, cww)]
-    holder = p // per_row
-
-    @pl.when(has_coupling)
-    def _():
-        @pl.loop(0, ns)
-        def _(t):
-            send_or_keep(t == s, hpart.at[t], hrecv.at[s], a1_send, a1_recv, i * ns + t, p)
-
-    @pl.when(q == holder)
-    def _():
-        @pl.loop(0, i * ns // 2)
-        def _(t):
-            send(piece, pk, a2_send, a2_recv, i * ns - 2 - 2 * t + core, p)
-
-    send_c2(0)
-
-    @pl.when(has_coupling)
-    def _():
-        wait(hrecv, a1_recv, "a1")
-        wait(pk, a2_recv, "a2")
-
-        @pl.when(core == holder % 2)
-        def _():
-            send(pk, pk, a2_pass, a2_recv, partner, p)
-
-        gpart[...] = dot3(pk[...], jnp.sum(hrecv[...], axis=0), COL_BY_COL)
-        for k in range(1, RB):
-
-            @pl.when(k_own == k)
-            def _(k=k):
-                dst = grecv.at[k - 1, w_own]
-                pltpu.make_async_copy(gpart.at[rows_of(p, fw)], dst, a3_recv[k - 1]).start()
-
-                @pl.loop(0, np_ - 1)
-                def _(d):
-                    to = far_first(d)
-                    send(gpart.at[rows_of(to, fw)], dst, a3_send, a3_recv[k - 1], q, to)
-
-    @pl.when(has_pair)
-    def _():
+    def send_b2():
         wait(bx, b1_recv, "bx")
         wait(qx, q1_recv, "qx")
         wait(ql, l1_recv, "ql")
@@ -262,7 +224,55 @@
             src, dst = tpart.at[:, t], trecv.at[z]
             send_or_keep(t == z, src, dst, b2_send, b2_recv, q, t * nx + x)
 
-    send_c3(0)
+    @pl.when(q == holder)
+    def _():
+        @pl.loop(0, i * ns // 2)
+        def _(t):
+            send(piece, pk, a2_send, a2_recv, i * ns - 2 - 2 * t + core, p)
+
+    @pl.when(has_coupling)
+    def _():
+        @pl.loop(0, ns)
+        def _(t):
+            send_or_keep(t == s, hpart.at[t], hrecv.at[s], a1_send, a1_recv, i * ns + t, p)
+
+    send_c1(0)
+    send_q2(0)
+    pl.when(early_pair)(send_b1)
+    send_c1(1)
+    send_q2(1)
+
+    @pl.when(has_coupling)
+    def _():
+        wait(hrecv, a1_recv, "a1")
+        wait(pk, a2_recv, "a2")
+
+        @pl.when(core == holder % 2)
+        def _():
+            send(pk, pk, a2_pass, a2_recv, partner, p)
+
+        gpart[...] = dot3(pk[...], jnp.sum(hrecv[...], axis=0), COL_BY_COL)
+        for k in range(1, RB):
+
+            @pl.when(k_own == k)
+            def _(k=k):
+                dst = grecv.at[k - 1, w_own]
+                pltpu.make_async_copy(gpart.at[rows_of(p, fw)], dst, a3_recv[k - 1]).start()
+
+                @pl.loop(0, np_ - 1)
+                def _(d):
+                    to = far_first(d)
+                    send(gpart.at[rows_of(to, fw)], dst, a3_send, a3_recv[k - 1], q, to)
+
+    send_c2(0)
+
+    @pl.when(top)
+    def _():
+        send_c3(0)
+
+    pl.when(late_pair)(send_b1)
+    pl.when(early_pair)(send_b2)
+    send_c2(1)
 
     for k in range(RB - 1, 0, -1):
 
@@ -276,6 +286,13 @@
             @pl.loop(0, np_ - 1)
             def _(d):
                 send(apiece.at[k - 1], dst, a4_send[k - 1], a4_recv[k - 1], q, far_first(d))
+
+    @pl.when(jnp.logical_not(top))
+    def _():
+        send_c3(0)
+
+    send_c3(1)
+    pl.when(late_pair)(send_b2)
 
     own_rows = rows_of(x * nz + z, fw)
 
@@ -303,73 +320,26 @@
 
         yrow[j, own_rows, :] = yown[j]
 
-    def left_terms(j):
-        for k in range(RB - 1, 0, -1):
-
-            @pl.when(k > i)
-            def _(k=k):
-                if j == 0:
-                    wait(at.at[k], a4_recv[k - 1], "a4_%d" % k)
-                wait(ycol.at[k - 1, j], col_recv[k - 1][j], "col_%d_%d" % (k, j))
-                acc[...] -= dot3(ycol[k - 1, j], at[k])
+    def left_term(j, k, total):
+        if j == 0:
+            wait(at.at[k], a4_recv[k - 1], "a4_%d" % k)
+        wait(ycol.at[k - 1, j], col_recv[k - 1][j], "col_%d_%d" % (k, j))
+        total[...] -= dot3(ycol[k - 1, j], at[k])
+
+    def older_left_terms(j, total):
+        for k in range(RB - 1, 1, -1):
+            pl.when(k > i + 1)(functools.partial(left_term, j, k, total))
+
+    def newest_left_term(j, total):
+        for k in range(1, RB):
+            pl.when(k == i + 1)(functools.partial(left_term, j, k, total))
 
     def last_product(j):
         wait(wbuf.at[j, :, pl.ds(0, (ns - 1) * ew)], w_recv[j], "wx_%d" % j)
         out[j] = dot3(wbuf[j], bases[...], ROW_BY_ROW)
 
-    wait(crecv.at[blocks[0]], c3_recv[0], "c3_0")
-    acc[...] = jnp.sum(crecv[0], axis=0)
-
-    @pl.when(i == RB - 1)
-    def _():
-        finish(0)
-
-    @pl.when(has_pair)
-    def _():
-        wait(trecv, b2_recv, "b2")
-        tpiece[...] = jnp.sum(trecv[...], axis=0)
-
-        for l in range(CB - 1):
-
-            @pl.when(l_own == l)
-            def _(l=l):
-                @pl.loop(0, nq * nx)
-                def _(t):
-                    q_to, x_to = nq - 1 - t // nx, t % nx
-                    dst = lhs.at[l, rows_of(j_own - l, fw), rows_of(x, ew)]
-                    here = jnp.logical_and(q_to == q, x_to == x)
-                    to = z * nx + x_to
-                    send_or_keep(here, tpiece.at[x_to], dst, b3_send, b3_recv[l], q_to, to)
-
-    send_c1(1)
-    send_q2(1)
-
-    @pl.when(i < RB - 1)
-    def _():
-        left_terms(0)
-        finish(0)
-
-    send_c2(1)
-    send_c3(1)
-    wait(crecv.at[blocks[1]], c3_recv[1], "c3_1")
-    for j in range(1, CB):
-        pend[j] = jnp.sum(crecv[j], axis=0)
-
-    for j in range(CB):
-        if j > 0:
-            acc[...] = pend[j]
-            left_terms(j)
-            finish(j)
-            last_product(j - 1)
-
-        wait(yrow.at[j, pl.ds(0, bs - fw)], row_recv[j], "row_%d" % j)
-        if j < CB - 1:
-            wait(lhs.at[j, fw : (CB - j) * fw], b3_recv[j], "b3_%d" % j)
-        both = dot3(lhs[j, : (CB - j) * fw], yrow[j])
-        wown[j] = both[:fw]
-        for later in range(j + 1, CB):
-            at_row = (later - j) * fw
-            pend[later] -= both[at_row : at_row + fw]
+    def exchange(j):
+        wown[j] = dot3(colbases[j], yrow[j])
         wbuf[j, :, own_lanes] = wown[j]
 
         @pl.loop(1, ns)
@@ -383,7 +353,71 @@
                 p,
             )
 
+    def pair_at(l, j):
+        return j * (j - 1) // 2 + l
+
+    def pass_pairs(j):
+        for l in range(j):
+            n = pair_at(l, j)
+            wait(lhs.at[n], b3_recv[n], "b3_%d" % n)
+
+            @pl.when(core == (nq - 1 - n) % 2)
+            def _(n=n):
+                send(lhs.at[n], lhs.at[n], b3_pass[n], b3_recv[n], partner, p)
+
+    wait(crecv.at[blocks[0]], c3_recv[0], "c3_0")
+    acc[...] = jnp.sum(crecv[0], axis=0)
+    older_left_terms(0, acc)
+    newest_left_term(0, acc)
+    finish(0)
+
+    @pl.when(has_pair)
+    def _():
+        wait(trecv, b2_recv, "b2")
+        tpiece[...] = jnp.sum(trecv[...], axis=0)
+        dst = lhs.at[pair, :, rows_of(x, ew)]
+        recv_sem = sems.at[b3_base + pair]
+
+        @pl.loop(0, nq // 2 * nx)
+        def _(t):
+            q_to, x_to = nq - 2 - t // nx * 2 + core, t % nx
+            here = jnp.logical_and(q_to == q, x_to == x)
+            to = z * nx + x_to
+            send_or_keep(here, tpiece.at[x_to], dst, b3_send, recv_sem, q_to, to)
+
+    wait(crecv.at[blocks[1]], c3_recv[1], "c3_1")
+    for j in range(1, CB):
+        pend[j] = jnp.sum(crecv[j], axis=0)
+
+    for j in range(CB):
+        if j == 0:
+            pass_pairs(1)
+        else:
+            exchange(j - 1)
+        if j + 2 < CB:
+            pass_pairs(j + 2)
+        if j + 1 < CB:
+            for l in range(j):
+                pend[j + 1] -= dot3(lhs[pair_at(l, j + 1)], yrow[l])
+            older_left_terms(j + 1, pend.at[j + 1])
+        if j > 1:
+            last_product(j - 2)
+
+        wait(yrow.at[j, pl.ds(0, bs - fw)], row_recv[j], "row_%d" % j)
+        if j + 1 < CB:
+            acc[...] = pend[j + 1] - dot3(lhs[pair_at(j, j + 1)], yrow[j])
+            newest_left_term(j + 1, acc)
+            finish(j + 1)
+
+    exchange(CB - 1)
+    last_product(CB - 2)
     last_product(CB - 1)
+
+    for n in range(PAIRS):
+
+        @pl.when(core == (nq - 1 - n) % 2)
+        def _(n=n):
+            wait(lhs.at[n], b3_pass[n])
 
     for c in range(2):
         wait(urecv.at[pl.ds(0, ns - 1), chunks[c]], c1_send[c])
@@ -424,7 +458,7 @@
         wait(qx.at[pl.ds(0, (nx - 1) * fw)], q1_send)
         wait(ql.at[pl.ds(0, bs - fw)], l1_send)
         wait(trecv.at[pl.ds(0, nz - 1)], b2_send)
-        wait(yrow.at[pl.ds(0, 2), pl.ds(0, (nq * nx - 1) * fw // 2)], b3_send)
+        wait(yrow.at[0, pl.ds(0, (nq // 2 * nx - 1) * fw)], b3_send)
 
 
 def shards(np_, nq, right_side, coupling, row_bases, row_values, column_bases, column_values, column_coupling):
@@ -457,7 +491,7 @@
         (nx, nz, fw, ew),
         (nz, nx, fw, ew),
         (nx, fw, ew),
-        (CB, CB * fw, bs),
+        (PAIRS, fw, bs),
         (CB, fw, ew),
         (CB, fw, ew),
         (CB, bs, ew),
@@ -473,7 +507,7 @@
         in_specs=[vmem] * 7,
         out_specs=vmem,
         scratch_shapes=[pltpu.VMEM(shape, F32) for shape in scratch]
-        + [pltpu.SemaphoreType.DMA((96,))],
+        + [pltpu.SemaphoreType.DMA((128,))],
         compiler_params=pltpu.CompilerParams(collective_id=0, has_side_effects=True),
     )(
         right_side,

time: 140 us -> 136 us (0.971)
  Pallas kernels: 138 us -> 134 us
    pallas_call x1, Pallas kernels: 138 us -> 134 us  [shards(): pl.pallas_call(functools.partial(kernel, np_, nq), out_shape=jax.ShapeDty...]
where the time goes in v4:
time: 136 us
  Pallas kernels  134 us (99%)
  local copies, waits for them, and re-layouts  1.42 us (1%)
    pallas_call x1, Pallas kernels, shards(): pl.pallas_call(functools.partial(kernel, np_, nq), out_shape=jax.ShapeDty...  134 us

profile of v4, /device:TPU:1, one launch (start us, length us, event | category | flops | bytes accessed | tf_op | source)
XLA Modules:
  0.0 135.6 jit_solution(11029150355994984472)
XLA Ops:
  0.0 134.1 %shard_map.73 = f32[6,16,128]{2,1,0:T(8,128)} custom-call(f32[6,16,128]{2,1,0:T(8,128)} %refs_0_.1, f32[64,128]{1,0:T(8,128)} %bitcast.1, f32[128,512]{1,0:T(8,128)} %refs_2_.1, f32[4,512]{1,0:T(4,128)} %refs_3_.1, f32[6,16,512]{2,1,0:T(8,128)} %refs_4_.1, f32[6,512]{1,0:T(8,128)} %refs_5_.1, f32[6,16,3072]{2,1,0:T(8,128)} %refs_6_.1), custom_call_target="tpu_custom_call" | custom-call | tf_op jit(solution)/shard_map/pallas_call | solution.py:504
  134.2 1.4 %copy.9 = f32[6,16,128]{2,1,0:T(8,128)} copy(f32[6,16,128]{2,1,0:T(8,128)} %shard_map.73) | data formatting | bytes 98304

commit v5 on v4

v5 whole, which is shorter than its diff:
```python
import functools

import jax
import jax.numpy as jnp
from jax import lax
from jax.experimental import pallas as pl
from jax.experimental.pallas import tpu as pltpu
from jax.sharding import PartitionSpec as P

RB = 4
CB = 6
PAIRS = CB * (CB - 1) // 2
MESH = pl.DeviceIdType.MESH
F32 = jnp.float32
BF16 = jnp.bfloat16
ROW_BY_COL = ((1,), (0,))
COL_BY_COL = ((0,), (0,))
ROW_BY_ROW = ((1,), (1,))


def halves(value):
    high = value.astype(BF16)
    low = (value - high.astype(F32)).astype(BF16)
    return high, low


def dot_of(left, right, dims):
    return lax.dot_general(left, right, (dims, ((), ())), preferred_element_type=F32)


def dot_split(left, right, dims):
    (left_high, left_low), (right_high, right_low) = left, right
    small = dot_of(left_low, right_high, dims) + dot_of(left_high, right_low, dims)
    return dot_of(left_high, right_high, dims) + small


def dot3(left, right, dims=ROW_BY_COL):
    return dot_split(halves(left), halves(right), dims)


def kernel(np_, nq, *refs):
    (rhs, coupling, bases, row_values, colbases, col_values, colcoup, out, *rest) = refs
    (upart, urecv, ux, uown, qside, vpart, crecv) = rest[:7]
    (hpart, hrecv, pk, gpart, grecv, apiece, at) = rest[7:14]
    (bx, qx, ql, tpart, trecv, tpiece, lhs) = rest[14:21]
    (yown, yx, xpart, brecv, wpart, wrecv, wown, wbuf) = rest[21:29]
    (ycol, pend, psum, den, acc, sems) = rest[29:]
    fw, ew = rhs.shape[1], rhs.shape[2]
    cww = coupling.shape[0]
    bs = fw * np_
    ns = nq // RB
    nx = bs // ew
    nz = np_ // nx
    nw = bs // cww
    per_row = ew // cww
    q = lax.axis_index("prow")
    p = lax.axis_index("pcol")
    i, s = q // ns, q % ns
    z, x = p // nx, p % nx
    core = q % 2
    partner = q + 1 - 2 * core
    k_own, w_own = p // nw, p % nw
    has_coupling = k_own > i
    top = i == RB - 1
    holder = p // per_row
    late_pair = jnp.logical_and(q > ns, q < nq - ns)

    used = [0]

    def new_sem(count=1):
        at_sem = used[0]
        used[0] += count
        return [sems.at[at_sem + n] for n in range(count)]

    z_send, z_recv, x_send, x_recv = new_sem(CB), new_sem(CB), new_sem(CB), new_sem(CB)
    v_send, v_recv = new_sem(CB), new_sem(CB)
    w_send, w_recv, col_send = new_sem(CB), new_sem(CB), new_sem(CB)
    col_recv = [new_sem(CB) for _ in range(RB - 1)]
    c1_send, c1_recv, c2_send, c2_recv = new_sem(2), new_sem(2), new_sem(2), new_sem(2)
    c3_send, c3_recv, q2_send, q2_recv = new_sem(2), new_sem(2), new_sem(2), new_sem(2)
    a1_send, a1_recv, a2_send, a2_recv, a2_pass, a3_send = new_sem(6)
    a3_recv, a4_send, a4_recv = new_sem(RB - 1), new_sem(RB - 1), new_sem(RB - 1)
    b1_send, b1_recv, q1_send, q1_recv = new_sem(2), new_sem(2), new_sem(2), new_sem(2)
    l1_send, l1_recv, b2_send, b2_recv = new_sem(2), new_sem(2), new_sem(2), new_sem(2)
    b3_send = new_sem(2)
    b3_pass = new_sem(PAIRS)
    b3_base = used[0]
    b3_recv = new_sem(PAIRS)

    def send(src, dst, send_sem, recv_sem, q_to, p_to):
        pltpu.make_async_remote_copy(
            src_ref=src,
            dst_ref=dst,
            send_sem=send_sem,
            recv_sem=recv_sem,
            device_id=(q_to, p_to),
            device_id_type=MESH,
        ).start()

    def keep(src, dst, recv_sem):
        pltpu.make_async_copy(src, dst, recv_sem).start()

    def send_or_keep(here, src, dst, send_sem, recv_sem, q_to, p_to):
        @pl.when(here)
        def _():
            keep(src, dst, recv_sem)

        @pl.when(jnp.logical_not(here))
        def _():
            send(src, dst, send_sem, recv_sem, q_to, p_to)

    def wait(ref, sem, name="w"):
        pltpu.make_async_copy(ref, ref, sem).wait()

    def rows_of(n, size):
        return pl.ds(pl.multiple_of(n * size, size), size)

    def to_columns(body):
        for start, stop in ((np_ // 2, np_), (1, np_ // 2)):

            @pl.loop(start, stop)
            def _(d):
                body(lax.rem(p + d, np_))

    def pair_of(n):
        j_own = 1
        for first in range(2, CB):
            j_own = j_own + (n >= first * (first - 1) // 2).astype(jnp.int32)
        return n - j_own * (j_own - 1) // 2, j_own

    own_pair = (nq - 1 - q, nq + ns - 1 - q)

    barrier = pltpu.get_barrier_semaphore()

    def greet(to):
        pl.semaphore_signal(barrier, inc=1, device_id=(q, to), device_id_type=MESH)

    to_columns(greet)

    @pl.loop(1, nq)
    def _(d):
        pl.semaphore_signal(
            barrier, inc=1, device_id=(lax.rem(q + d, nq), p), device_id_type=MESH
        )

    bases_split = halves(bases[...])
    inner = dot_split(halves(coupling[...]), bases_split, ROW_BY_COL)
    stacked = rhs[...].reshape(CB * fw, ew)
    first = dot_split(halves(stacked), bases_split, ROW_BY_COL)
    for n in range(ns):
        upart[n] = first[:, n * ew : (n + 1) * ew]
        hpart[n] = inner[:, n * ew : (n + 1) * ew]
    own_lanes = rows_of(s, ew)
    values = row_values[:, own_lanes]
    own_value = lax.broadcasted_iota(jnp.int32, values.shape, 0) == i
    eigen = jnp.sum(jnp.where(own_value, values, 0.0), axis=0, keepdims=True)
    lanes = lax.broadcasted_iota(jnp.int32, (fw, ew), 1)
    chosen = lanes == z * fw + lax.broadcasted_iota(jnp.int32, (fw, ew), 0)
    for j in range(CB):
        shifts = col_values[pl.ds(j, 1), rows_of(x, ew)]
        shift = jnp.sum(jnp.where(chosen, shifts, 0.0), axis=1, keepdims=True)
        den[j] = shift + eigen

    pl.semaphore_wait(barrier, np_ + nq - 2)

    chunks = (pl.ds(0, fw), pl.ds(fw, (CB - 1) * fw))
    blocks = (pl.ds(0, 1), pl.ds(1, CB - 1))

    def send_c1(c):
        @pl.loop(0, ns)
        def _(t):
            src, dst = upart.at[t, chunks[c]], urecv.at[s, chunks[c]]
            send_or_keep(t == s, src, dst, c1_send[c], c1_recv[c], i * ns + t, p)

    def send_q2(c):
        @pl.loop(0, nx)
        def _(t):
            src, dst = colbases.at[blocks[c], :, rows_of(t, ew)], qside.at[blocks[c], x]
            send_or_keep(t == x, src, dst, q2_send[c], q2_recv[c], q, z * nx + t)

    def send_c2(c):
        wait(urecv.at[:, chunks[c]], c1_recv[c], "c1_%d" % c)
        count = (1, CB - 1)[c]
        summed = jnp.sum(urecv[:, chunks[c]], axis=0)
        uown[blocks[c]] = summed.reshape(count, fw, ew)

        @pl.loop(0, nx)
        def _(t):
            src, dst = uown.at[blocks[c]], ux.at[blocks[c], x]
            send_or_keep(t == x, src, dst, c2_send[c], c2_recv[c], q, z * nx + t)

    def send_c3(c):
        wait(ux.at[blocks[c]], c2_recv[c], "c2_%d" % c)
        wait(qside.at[blocks[c]], q2_recv[c], "q2_%d" % c)
        for j in ((0,), tuple(range(1, CB)))[c]:
            left = qside[j].reshape(nx * fw, ew)
            right = ux[j].reshape(nx * fw, ew)
            vpart[j] = dot3(left, right, COL_BY_COL).reshape(nz, fw, ew)

        @pl.loop(0, nz)
        def _(t):
            src, dst = vpart.at[blocks[c], t], crecv.at[blocks[c], z]
            send_or_keep(t == z, src, dst, c3_send[c], c3_recv[c], q, t * nx + x)

    def send_b1(r, n):
        l_own, j_own = pair_of(n)

        @pl.loop(0, nx)
        def _(t):
            src_b = colcoup.at[j_own, :, rows_of(l_own, bs)]
            src_q = colbases.at[j_own]
            dst_b, dst_q = bx.at[r, rows_of(x, fw)], qx.at[r, rows_of(x, fw)]
            to = z * nx + t
            send_or_keep(t == x, src_b, dst_b, b1_send[r], b1_recv[r], q, to)
            send_or_keep(t == x, src_q, dst_q, q1_send[r], q1_recv[r], q, to)

        dst = ql.at[r, rows_of(p, fw)]
        keep(colbases.at[l_own, :, rows_of(x, ew)], dst, l1_recv[r])

        def one(to):
            src = colbases.at[l_own, :, rows_of(lax.rem(to, nx), ew)]
            send(src, dst, l1_send[r], l1_recv[r], q, to)

        to_columns(one)

    def send_b2(r):
        wait(bx.at[r], b1_recv[r], "bx%d" % r)
        wait(qx.at[r], q1_recv[r], "qx%d" % r)
        wait(ql.at[r], l1_recv[r], "ql%d" % r)
        mixed = dot3(bx[r], ql[r])
        tpart[r] = dot3(qx[r], mixed, COL_BY_COL).reshape(nx, nz, fw, ew)

        @pl.loop(0, nz)
        def _(t):
            src, dst = tpart.at[r, :, t], trecv.at[r, z]
            send_or_keep(t == z, src, dst, b2_send[r], b2_recv[r], q, t * nx + x)

    def send_b3(r, n):
        wait(trecv.at[r], b2_recv[r], "b2%d" % r)
        tpiece[r] = jnp.sum(trecv[r], axis=0)
        dst, recv_sem = lhs.at[n], sems.at[b3_base + n]

        @pl.loop(0, nq // 2)
        def _(t):
            q_to = nq - 2 - 2 * t + core
            send_or_keep(q_to == q, tpiece.at[r], dst, b3_send[r], recv_sem, q_to, p)

    @pl.when(q == holder)
    def _():
        @pl.loop(0, i * ns // 2)
        def _(t):
            src = bases.at[rows_of(lax.rem(p, per_row), cww)]
            send(src, pk, a2_send, a2_recv, i * ns - 2 - 2 * t + core, p)

    @pl.when(has_coupling)
    def _():
        @pl.loop(0, ns)
        def _(t):
            send_or_keep(t == s, hpart.at[t], hrecv.at[s], a1_send, a1_recv, i * ns + t, p)

    send_c1(0)
    send_q2(0)

    @pl.when(top)
    def _():
        send_b1(0, own_pair[0])

    send_c1(1)
    send_q2(1)

    @pl.when(has_coupling)
    def _():
        wait(hrecv, a1_recv, "a1")
        wait(pk, a2_recv, "a2")

        @pl.when(core == holder % 2)
        def _():
            send(pk, pk, a2_pass, a2_recv, partner, p)

        gpart[...] = dot3(pk[...], jnp.sum(hrecv[...], axis=0), COL_BY_COL)
        for k in range(1, RB):

            @pl.when(k_own == k)
            def _(k=k):
                dst = grecv.at[k - 1, w_own]
                keep(gpart.at[rows_of(p, fw)], dst, a3_recv[k - 1])

                def one(to):
                    send(gpart.at[rows_of(to, fw)], dst, a3_send, a3_recv[k - 1], q, to)

                to_columns(one)

    send_c2(0)
    send_c3(0)

    @pl.when(top)
    def _():
        send_b2(0)
        send_b1(1, own_pair[1])

    send_c2(1)

    for k in range(RB - 1, 0, -1):

        @pl.when(k > i)
        def _(k=k):
            wait(grecv.at[k - 1], a3_recv[k - 1], "a3_%d" % k)
            apiece[k - 1] = jnp.sum(grecv[k - 1], axis=0)
            dst = at.at[k, rows_of(p, fw)]
            keep(apiece.at[k - 1], dst, a4_recv[k - 1])

            def one(to):
                send(apiece.at[k - 1], dst, a4_send[k - 1], a4_recv[k - 1], q, to)

            to_columns(one)

    send_c3(1)

    @pl.when(late_pair)
    def _():
        send_b1(0, own_pair[1])

    def finish(j):
        yown[j] = acc[...] / den[j]
        for d in (4, 3, 5, 2, 6, 1, 7):
            if d < nz:
                to = lax.rem(z + d, nz) * nx + x
                send(yown.at[j], yx.at[j, z], z_send[j], z_recv[j], q, to)
        for k in range(1, RB):

            @pl.when(i == k)
            def _(k=k):
                @pl.loop(0, k * ns)
                def _(t):
                    send(
                        yown.at[j],
                        ycol.at[k - 1, j, :, own_lanes],
                        col_send[j],
                        col_recv[k - 1][j],
                        k * ns - 1 - t,
                        p,
                    )

        yx[j, z] = yown[j]

    def left_term(j, k, total):
        if j == 0:
            wait(at.at[k], a4_recv[k - 1], "a4_%d" % k)
        wait(ycol.at[k - 1, j], col_recv[k - 1][j], "col_%d_%d" % (k, j))
        total[...] -= dot3(ycol[k - 1, j], at[k])

    def older_left_terms(j, total):
        for k in range(RB - 1, 1, -1):
            pl.when(k > i + 1)(functools.partial(left_term, j, k, total))

    def newest_left_term(j, total):
        for k in range(1, RB):
            pl.when(k == i + 1)(functools.partial(left_term, j, k, total))

    def scatter_x(part, arrived, send_sem, recv_sem):
        for d in (2, 1, 3):
            if d < nx:
                to = lax.rem(x + d, nx)
                send(part.at[to], arrived.at[x], send_sem, recv_sem, q, z * nx + to)

    def whole_of(ref, j):
        return ref[j].reshape(nz * fw, ew)

    def start_last(j):
        wpart[j] = dot3(qside[j].reshape(nx * fw, ew), whole_of(yx, j)).reshape(nx, fw, ew)
        scatter_x(wpart.at[j], wrecv.at[j], v_send[j], v_recv[j])
        wrecv[j, x] = wpart[j, x]

    def exchange(j):
        wait(wrecv.at[j, pl.ds(0, nx - 1)], v_recv[j], "v_%d" % j)
        wown[j] = jnp.sum(wrecv[j], axis=0)

        @pl.loop(1, ns)
        def _(d):
            send(
                wown.at[j],
                wbuf.at[j, :, own_lanes],
                w_send[j],
                w_recv[j],
                i * ns + lax.rem(s + d, ns),
                p,
            )

        wbuf[j, :, own_lanes] = wown[j]

    def last_product(j):
        wait(wbuf.at[j, :, pl.ds(0, (ns - 1) * ew)], w_recv[j], "wx_%d" % j)
        out[j] = dot3(wbuf[j], bases[...], ROW_BY_ROW)

    def pair_at(l, j):
        return j * (j - 1) // 2 + l

    def pass_pairs(j):
        for l in range(j):
            n = pair_at(l, j)

            @pl.when(core == (nq - 1 - n) % 2)
            def _(n=n):
                wait(lhs.at[n], b3_recv[n], "b3_%d" % n)
                send(lhs.at[n], lhs.at[n], b3_pass[n], b3_recv[n], partner, p)

        for l in range(j):
            n = pair_at(l, j)

            @pl.when(core != (nq - 1 - n) % 2)
            def _(n=n):
                wait(lhs.at[n], b3_recv[n], "b3_%d" % n)

    def right_term(l, j):
        return dot3(lhs[pair_at(l, j)].reshape(nx * fw, ew), whole_of(yx, l))

    wait(crecv.at[blocks[0]], c3_recv[0], "c3_0")
    acc[...] = jnp.sum(crecv[0], axis=0)
    older_left_terms(0, acc)
    newest_left_term(0, acc)
    finish(0)

    @pl.when(top)
    def _():
        send_b3(0, own_pair[0])
        send_b2(1)

    wait(crecv.at[blocks[1]], c3_recv[1], "c3_1")
    for j in range(1, CB):
        pend[j] = jnp.sum(crecv[j], axis=0)

    for j in range(CB):
        last = j + 1 == CB
        if not last:
            pass_pairs(j + 1)
            psum[...] = jnp.zeros_like(psum)
            for l in range(j):
                psum[...] += right_term(l, j + 1)
            older_left_terms(j + 1, pend.at[j + 1])
        if j >= 1:
            start_last(j - 1)
        if j >= 2:
            exchange(j - 2)
        if j >= 3:
            last_product(j - 3)
        if j == 0:
            pl.when(late_pair)(functools.partial(send_b2, 0))
        if j == 1:
            pl.when(top)(functools.partial(send_b3, 1, own_pair[1]))
        if j == 2:
            pl.when(late_pair)(functools.partial(send_b3, 0, own_pair[1]))

        wait(yx.at[j, pl.ds(0, nz - 1)], z_recv[j], "z_%d" % j)
        if not last:
            xpart[j + 1] = (psum[...] + right_term(j, j + 1)).reshape(nx, fw, ew)
            scatter_x(xpart.at[j + 1], brecv.at[j + 1], x_send[j + 1], x_recv[j + 1])
            brecv[j + 1, x] = xpart[j + 1, x]
            newest_left_term(j + 1, pend.at[j + 1])
            wait(brecv.at[j + 1, pl.ds(0, nx - 1)], x_recv[j + 1], "x_%d" % (j + 1))
            acc[...] = pend[j + 1] - jnp.sum(brecv[j + 1], axis=0)
            finish(j + 1)

    start_last(CB - 1)
    exchange(CB - 2)
    last_product(CB - 3)
    exchange(CB - 1)
    last_product(CB - 2)
    last_product(CB - 1)

    for n in range(PAIRS):

        @pl.when(core == (nq - 1 - n) % 2)
        def _(n=n):
            wait(lhs.at[n], b3_pass[n])

    for c in range(2):
        wait(urecv.at[pl.ds(0, ns - 1), chunks[c]], c1_send[c])
        wait(ux.at[blocks[c], pl.ds(0, nx - 1)], c2_send[c])
        wait(qside.at[blocks[c], pl.ds(0, nx - 1)], q2_send[c])
        wait(crecv.at[blocks[c], pl.ds(0, nz - 1)], c3_send[c])
    for j in range(CB):
        wait(yx.at[j, pl.ds(0, nz - 1)], z_send[j])
        wait(wrecv.at[j, pl.ds(0, nx - 1)], v_send[j])
        wait(wbuf.at[j, :, pl.ds(0, (ns - 1) * ew)], w_send[j])
        if j > 0:
            wait(brecv.at[j, pl.ds(0, nx - 1)], x_send[j])
        for k in range(1, RB):

            @pl.when(i == k)
            def _(k=k):
                wait(at.at[0, pl.ds(0, fw * k * ns)], col_send[j])

    for k in range(1, RB):

        @pl.when(k > i)
        def _(k=k):
            wait(at.at[k, pl.ds(0, bs - fw)], a4_send[k - 1])

        @pl.when(jnp.logical_and(i == k, q == holder))
        def _(k=k):
            wait(at.at[pl.ds(0, k * ns * cww // (2 * ew))], a2_send)

    @pl.when(has_coupling)
    def _():
        wait(hrecv.at[pl.ds(0, ns - 1)], a1_send)
        wait(gpart.at[pl.ds(0, bs - fw)], a3_send)

        @pl.when(core == holder % 2)
        def _():
            wait(pk, a2_pass)

    def end_pair(r):
        wait(bx.at[r, pl.ds(0, (nx - 1) * fw)], b1_send[r])
        wait(qx.at[r, pl.ds(0, (nx - 1) * fw)], q1_send[r])
        wait(ql.at[r, pl.ds(0, bs - fw)], l1_send[r])
        wait(trecv.at[r, pl.ds(0, nz - 1)], b2_send[r])
        wait(at.at[0, pl.ds(0, (nq // 2 - 1) * nx * fw)], b3_send[r])

    @pl.when(top)
    def _():
        end_pair(0)
        end_pair(1)

    pl.when(late_pair)(functools.partial(end_pair, 0))


def shards(np_, nq, right_side, coupling, row_bases, row_values, column_bases, column_values, column_coupling):
    ns = nq // RB
    fw, ew = right_side.shape[1], right_side.shape[2]
    cww = coupling.shape[1]
    bs = row_bases.shape[1]
    nx = bs // ew
    nz = np_ // nx
    nw = bs // cww
    vmem = pl.BlockSpec(memory_space=pltpu.VMEM)
    scratch = (
        (ns, CB * fw, ew),
        (ns, CB * fw, ew),
        (CB, nx, fw, ew),
        (CB, fw, ew),
        (CB, nx, fw, ew),
        (CB, nz, fw, ew),
        (CB, nz, fw, ew),
        (ns, cww, ew),
        (ns, cww, ew),
        (cww, bs),
        (bs, ew),
        (RB - 1, nw, fw, ew),
        (RB - 1, fw, ew),
        (RB, bs, ew),
        (2, nx * fw, bs),
        (2, nx * fw, bs),
        (2, bs, ew),
        (2, nx, nz, fw, ew),
        (2, nz, nx, fw, ew),
        (2, nx, fw, ew),
        (PAIRS, nx, fw, ew),
        (CB, fw, ew),
        (CB, nz, fw, ew),
        (CB, nx, fw, ew),
        (CB, nx, fw, ew),
        (CB, nx, fw, ew),
        (CB, nx, fw, ew),
        (CB, fw, ew),
        (CB, fw, bs),
        (RB - 1, CB, fw, bs),
        (CB, fw, ew),
        (nx * fw, ew),
        (CB, fw, ew),
        (fw, ew),
    )
    return pl.pallas_call(
        functools.partial(kernel, np_, nq),
        out_shape=jax.ShapeDtypeStruct((CB, fw, ew), F32),
        in_specs=[vmem] * 7,
        out_specs=vmem,
        scratch_shapes=[pltpu.VMEM(shape, F32) for shape in scratch]
        + [pltpu.SemaphoreType.DMA((160,))],
        compiler_params=pltpu.CompilerParams(collective_id=0, has_side_effects=True),
    )(
        right_side,
        coupling.T,
        row_bases,
        row_values,
        column_bases,
        column_values,
        column_coupling,
    )


def solution(mesh):
    placed = (
        P(None, "pcol", "prow"),
        P("prow", "pcol"),
        P("prow", None),
        P(),
        P(None, "pcol", None),
        P(),
        P(None, "pcol", None),
    )
    body = functools.partial(shards, mesh.shape["pcol"], mesh.shape["prow"])
    return jax.shard_map(
        body, mesh=mesh, in_specs=placed, out_specs=P(None, "pcol", "prow"), check_vma=False
    )
```

time: 136 us -> 122 us (0.90)
  Pallas kernels: 134 us -> 121 us
    pallas_call x1, Pallas kernels: 134 us -> 121 us  [shards(): pl.pallas_call(functools.partial(kernel, np_, nq), out_shape=jax.ShapeDty...]
where the time goes in v5:
time: 122 us
  Pallas kernels  121 us (99%)
  local copies, waits for them, and re-layouts  1.42 us (1%)
    pallas_call x1, Pallas kernels, shards(): pl.pallas_call(functools.partial(kernel, np_, nq), out_shape=jax.ShapeDty...  121 us

profile of v5, /device:TPU:1, one launch (start us, length us, event | category | flops | bytes accessed | tf_op | source)
XLA Modules:
  0.0 122.0 jit_solution(14118193951791824658)
XLA Ops:
  0.0 120.5 %shard_map.73 = f32[6,16,128]{2,1,0:T(8,128)} custom-call(f32[6,16,128]{2,1,0:T(8,128)} %refs_0_.1, f32[64,128]{1,0:T(8,128)} %bitcast.1, f32[128,512]{1,0:T(8,128)} %refs_2_.1, f32[4,512]{1,0:T(4,128)} %refs_3_.1, f32[6,16,512]{2,1,0:T(8,128)} %refs_4_.1, f32[6,512]{1,0:T(8,128)} %refs_5_.1, f32[6,16,3072]{2,1,0:T(8,128)} %refs_6_.1), custom_call_target="tpu_custom_call" | custom-call | tf_op jit(solution)/shard_map/pallas_call | solution.py:572
  120.5 1.4 %copy.9 = f32[6,16,128]{2,1,0:T(8,128)} copy(f32[6,16,128]{2,1,0:T(8,128)} %shard_map.73) | data formatting | bytes 98304

commit v6 on v5

--- a/solution.py
+++ b/solution.py
@@ -10,6 +10,7 @@
 RB = 4
 CB = 6
 PAIRS = CB * (CB - 1) // 2
+FIRST = 2
 MESH = pl.DeviceIdType.MESH
 F32 = jnp.float32
 BF16 = jnp.bfloat16
@@ -80,6 +81,7 @@
     c3_send, c3_recv, q2_send, q2_recv = new_sem(2), new_sem(2), new_sem(2), new_sem(2)
     a1_send, a1_recv, a2_send, a2_recv, a2_pass, a3_send = new_sem(6)
     a3_recv, a4_send, a4_recv = new_sem(RB - 1), new_sem(RB - 1), new_sem(RB - 1)
+    a5_send, a5_recv = new_sem(RB - 1), new_sem(RB - 1)
     b1_send, b1_recv, q1_send, q1_recv = new_sem(2), new_sem(2), new_sem(2), new_sem(2)
     l1_send, l1_recv, b2_send, b2_recv = new_sem(2), new_sem(2), new_sem(2), new_sem(2)
     b3_send = new_sem(2)
@@ -163,8 +165,8 @@
 
     pl.semaphore_wait(barrier, np_ + nq - 2)
 
-    chunks = (pl.ds(0, fw), pl.ds(fw, (CB - 1) * fw))
-    blocks = (pl.ds(0, 1), pl.ds(1, CB - 1))
+    chunks = (pl.ds(0, FIRST * fw), pl.ds(FIRST * fw, (CB - FIRST) * fw))
+    blocks = (pl.ds(0, FIRST), pl.ds(FIRST, CB - FIRST))
 
     def send_c1(c):
         @pl.loop(0, ns)
@@ -180,7 +182,7 @@
 
     def send_c2(c):
         wait(urecv.at[:, chunks[c]], c1_recv[c], "c1_%d" % c)
-        count = (1, CB - 1)[c]
+        count = (FIRST, CB - FIRST)[c]
         summed = jnp.sum(urecv[:, chunks[c]], axis=0)
         uown[blocks[c]] = summed.reshape(count, fw, ew)
 
@@ -192,7 +194,7 @@
     def send_c3(c):
         wait(ux.at[blocks[c]], c2_recv[c], "c2_%d" % c)
         wait(qside.at[blocks[c]], q2_recv[c], "q2_%d" % c)
-        for j in ((0,), tuple(range(1, CB)))[c]:
+        for j in (range(FIRST), range(FIRST, CB))[c]:
             left = qside[j].reshape(nx * fw, ew)
             right = ux[j].reshape(nx * fw, ew)
             vpart[j] = dot3(left, right, COL_BY_COL).reshape(nz, fw, ew)
@@ -283,21 +285,21 @@
             @pl.when(k_own == k)
             def _(k=k):
                 dst = grecv.at[k - 1, w_own]
-                keep(gpart.at[rows_of(p, fw)], dst, a3_recv[k - 1])
+                keep(gpart.at[rows_of(x * nz + z, fw)], dst, a3_recv[k - 1])
 
                 def one(to):
-                    send(gpart.at[rows_of(to, fw)], dst, a3_send, a3_recv[k - 1], q, to)
+                    order = lax.rem(to, nx) * nz + to // nx
+                    send(gpart.at[rows_of(order, fw)], dst, a3_send, a3_recv[k - 1], q, to)
 
                 to_columns(one)
 
     send_c2(0)
+
+    @pl.when(top)
+    def _():
+        send_b2(0)
+
     send_c3(0)
-
-    @pl.when(top)
-    def _():
-        send_b2(0)
-        send_b1(1, own_pair[1])
-
     send_c2(1)
 
     for k in range(RB - 1, 0, -1):
@@ -306,15 +308,29 @@
         def _(k=k):
             wait(grecv.at[k - 1], a3_recv[k - 1], "a3_%d" % k)
             apiece[k - 1] = jnp.sum(grecv[k - 1], axis=0)
-            dst = at.at[k, rows_of(p, fw)]
+            dst = at.at[k, rows_of(x * nz + z, fw)]
             keep(apiece.at[k - 1], dst, a4_recv[k - 1])
-
-            def one(to):
-                send(apiece.at[k - 1], dst, a4_send[k - 1], a4_recv[k - 1], q, to)
-
-            to_columns(one)
+            for d in (4, 3, 5, 2, 6, 1, 7):
+                if d < nz:
+                    to = lax.rem(z + d, nz) * nx + x
+                    send(apiece.at[k - 1], dst, a4_send[k - 1], a4_recv[k - 1], q, to)
+
+    for k in range(RB - 1, 0, -1):
+
+        @pl.when(k > i)
+        def _(k=k):
+            half = at.at[k, rows_of(x, nz * fw)]
+            wait(half, a4_recv[k - 1], "a4_%d" % k)
+            for d in (2, 1, 3):
+                if d < nx:
+                    to = z * nx + lax.rem(x + d, nx)
+                    send(half, half, a5_send[k - 1], a5_recv[k - 1], q, to)
 
     send_c3(1)
+
+    @pl.when(top)
+    def _():
+        send_b1(1, own_pair[1])
 
     @pl.when(late_pair)
     def _():
@@ -345,7 +361,7 @@
 
     def left_term(j, k, total):
         if j == 0:
-            wait(at.at[k], a4_recv[k - 1], "a4_%d" % k)
+            wait(at.at[k, pl.ds(0, (nx - 1) * nz * fw)], a5_recv[k - 1], "a5_%d" % k)
         wait(ycol.at[k - 1, j], col_recv[k - 1][j], "col_%d_%d" % (k, j))
         total[...] -= dot3(ycol[k - 1, j], at[k])
 
@@ -423,14 +439,20 @@
     @pl.when(top)
     def _():
         send_b3(0, own_pair[0])
-        send_b2(1)
-
-    wait(crecv.at[blocks[1]], c3_recv[1], "c3_1")
-    for j in range(1, CB):
+
+    for j in range(1, FIRST):
         pend[j] = jnp.sum(crecv[j], axis=0)
 
     for j in range(CB):
         last = j + 1 == CB
+        if j == 1:
+            pl.when(top)(functools.partial(send_b2, 1))
+            pl.when(late_pair)(functools.partial(send_b2, 0))
+            wait(crecv.at[blocks[1]], c3_recv[1], "c3_1")
+            for later in range(FIRST, CB):
+                pend[later] = jnp.sum(crecv[later], axis=0)
+        if j == 2:
+            pl.when(top)(functools.partial(send_b3, 1, own_pair[1]))
         if not last:
             pass_pairs(j + 1)
             psum[...] = jnp.zeros_like(psum)
@@ -443,10 +465,8 @@
             exchange(j - 2)
         if j >= 3:
             last_product(j - 3)
-        if j == 0:
-            pl.when(late_pair)(functools.partial(send_b2, 0))
-        if j == 1:
-            pl.when(top)(functools.partial(send_b3, 1, own_pair[1]))
+        if last:
+            exchange(j - 1)
         if j == 2:
             pl.when(late_pair)(functools.partial(send_b3, 0, own_pair[1]))
 
@@ -461,10 +481,9 @@
             finish(j + 1)
 
     start_last(CB - 1)
-    exchange(CB - 2)
     last_product(CB - 3)
+    last_product(CB - 2)
     exchange(CB - 1)
-    last_product(CB - 2)
     last_product(CB - 1)
 
     for n in range(PAIRS):
@@ -494,7 +513,8 @@
 
         @pl.when(k > i)
         def _(k=k):
-            wait(at.at[k, pl.ds(0, bs - fw)], a4_send[k - 1])
+            wait(at.at[k, pl.ds(0, (nz - 1) * fw)], a4_send[k - 1])
+            wait(at.at[k, pl.ds(0, (nx - 1) * nz * fw)], a5_send[k - 1])
 
         @pl.when(jnp.logical_and(i == k, q == holder))
         def _(k=k):

time: 122 us -> 118 us (0.967)
  Pallas kernels: 121 us -> 116 us
    pallas_call x1, Pallas kernels: 121 us -> 116 us  [shards(): pl.pallas_call(functools.partial(kernel, np_, nq), out_shape=jax.ShapeDty...]
where the time goes in v6:
time: 118 us
  Pallas kernels  116 us (98%)
  local copies, waits for them, and re-layouts  1.42 us (1%)
    pallas_call x1, Pallas kernels, shards(): pl.pallas_call(functools.partial(kernel, np_, nq), out_shape=jax.ShapeDty...  116 us

profile of v6, /device:TPU:1, one launch (start us, length us, event | category | flops | bytes accessed | tf_op | source)
XLA Modules:
  0.0 117.8 jit_solution(8264916417490463782)
XLA Ops:
  0.0 116.3 %shard_map.73 = f32[6,16,128]{2,1,0:T(8,128)} custom-call(f32[6,16,128]{2,1,0:T(8,128)} %refs_0_.1, f32[64,128]{1,0:T(8,128)} %bitcast.1, f32[128,512]{1,0:T(8,128)} %refs_2_.1, f32[4,512]{1,0:T(4,128)} %refs_3_.1, f32[6,16,512]{2,1,0:T(8,128)} %refs_4_.1, f32[6,512]{1,0:T(8,128)} %refs_5_.1, f32[6,16,3072]{2,1,0:T(8,128)} %refs_6_.1), custom_call_target="tpu_custom_call" | custom-call | tf_op jit(solution)/shard_map/pallas_call | solution.py:592
  116.3 1.4 %copy.9 = f32[6,16,128]{2,1,0:T(8,128)} copy(f32[6,16,128]{2,1,0:T(8,128)} %shard_map.73) | data formatting | bytes 98304

commit v7 on v6

--- a/solution.py
+++ b/solution.py
@@ -44,8 +44,8 @@
     (upart, urecv, ux, uown, qside, vpart, crecv) = rest[:7]
     (hpart, hrecv, pk, gpart, grecv, apiece, at) = rest[7:14]
     (bx, qx, ql, tpart, trecv, tpiece, lhs) = rest[14:21]
-    (yown, yx, xpart, brecv, wpart, wrecv, wown, wbuf) = rest[21:29]
-    (ycol, pend, psum, den, acc, sems) = rest[29:]
+    (yown, yx, xpart, brecv, wpart, wrecv) = rest[21:27]
+    (ycol, pend, psum, den, acc, sems) = rest[27:]
     fw, ew = rhs.shape[1], rhs.shape[2]
     cww = coupling.shape[0]
     bs = fw * np_
@@ -74,7 +74,6 @@
         return [sems.at[at_sem + n] for n in range(count)]
 
     z_send, z_recv, x_send, x_recv = new_sem(CB), new_sem(CB), new_sem(CB), new_sem(CB)
-    v_send, v_recv = new_sem(CB), new_sem(CB)
     w_send, w_recv, col_send = new_sem(CB), new_sem(CB), new_sem(CB)
     col_recv = [new_sem(CB) for _ in range(RB - 1)]
     c1_send, c1_recv, c2_send, c2_recv = new_sem(2), new_sem(2), new_sem(2), new_sem(2)
@@ -144,6 +143,13 @@
         pl.semaphore_signal(
             barrier, inc=1, device_id=(lax.rem(q + d, nq), p), device_id_type=MESH
         )
+
+    @pl.loop(1, ns)
+    def _(d):
+        q_to = i * ns + lax.rem(s + d, ns)
+        for x_off in range(1, nx):
+            to = z * nx + lax.rem(x + x_off, nx)
+            pl.semaphore_signal(barrier, inc=1, device_id=(q_to, to), device_id_type=MESH)
 
     bases_split = halves(bases[...])
     inner = dot_split(halves(coupling[...]), bases_split, ROW_BY_COL)
@@ -163,7 +169,7 @@
         shift = jnp.sum(jnp.where(chosen, shifts, 0.0), axis=1, keepdims=True)
         den[j] = shift + eigen
 
-    pl.semaphore_wait(barrier, np_ + nq - 2)
+    pl.semaphore_wait(barrier, np_ + nq - 2 + (ns - 1) * (nx - 1))
 
     chunks = (pl.ds(0, FIRST * fw), pl.ds(FIRST * fw, (CB - FIRST) * fw))
     blocks = (pl.ds(0, FIRST), pl.ds(FIRST, CB - FIRST))
@@ -294,12 +300,12 @@
                 to_columns(one)
 
     send_c2(0)
+    send_c3(0)
 
     @pl.when(top)
     def _():
         send_b2(0)
 
-    send_c3(0)
     send_c2(1)
 
     for k in range(RB - 1, 0, -1):
@@ -325,16 +331,6 @@
                 if d < nx:
                     to = z * nx + lax.rem(x + d, nx)
                     send(half, half, a5_send[k - 1], a5_recv[k - 1], q, to)
-
-    send_c3(1)
-
-    @pl.when(top)
-    def _():
-        send_b1(1, own_pair[1])
-
-    @pl.when(late_pair)
-    def _():
-        send_b1(0, own_pair[1])
 
     def finish(j):
         yown[j] = acc[...] / den[j]
@@ -382,31 +378,25 @@
     def whole_of(ref, j):
         return ref[j].reshape(nz * fw, ew)
 
-    def start_last(j):
+    def exchange(j):
         wpart[j] = dot3(qside[j].reshape(nx * fw, ew), whole_of(yx, j)).reshape(nx, fw, ew)
-        scatter_x(wpart.at[j], wrecv.at[j], v_send[j], v_recv[j])
-        wrecv[j, x] = wpart[j, x]
-
-    def exchange(j):
-        wait(wrecv.at[j, pl.ds(0, nx - 1)], v_recv[j], "v_%d" % j)
-        wown[j] = jnp.sum(wrecv[j], axis=0)
+        dst = wrecv.at[j, x, :, own_lanes]
 
         @pl.loop(1, ns)
         def _(d):
-            send(
-                wown.at[j],
-                wbuf.at[j, :, own_lanes],
-                w_send[j],
-                w_recv[j],
-                i * ns + lax.rem(s + d, ns),
-                p,
-            )
-
-        wbuf[j, :, own_lanes] = wown[j]
+            q_to = i * ns + lax.rem(s + d, ns)
+            for x_to in range(nx):
+                send(wpart.at[j, x_to], dst, w_send[j], w_recv[j], q_to, z * nx + x_to)
+
+        for d in (2, 1, 3):
+            if d < nx:
+                to = lax.rem(x + d, nx)
+                send(wpart.at[j, to], dst, w_send[j], w_recv[j], q, z * nx + to)
+        keep(wpart.at[j, x], dst, w_recv[j])
 
     def last_product(j):
-        wait(wbuf.at[j, :, pl.ds(0, (ns - 1) * ew)], w_recv[j], "wx_%d" % j)
-        out[j] = dot3(wbuf[j], bases[...], ROW_BY_ROW)
+        wait(wrecv.at[j], w_recv[j], "wx_%d" % j)
+        out[j] = dot3(jnp.sum(wrecv[j], axis=0), bases[...], ROW_BY_ROW)
 
     def pair_at(l, j):
         return j * (j - 1) // 2 + l
@@ -430,15 +420,32 @@
     def right_term(l, j):
         return dot3(lhs[pair_at(l, j)].reshape(nx * fw, ew), whole_of(yx, l))
 
-    wait(crecv.at[blocks[0]], c3_recv[0], "c3_0")
-    acc[...] = jnp.sum(crecv[0], axis=0)
-    older_left_terms(0, acc)
-    newest_left_term(0, acc)
-    finish(0)
+    def start_rows():
+        wait(crecv.at[blocks[0]], c3_recv[0], "c3_0")
+        acc[...] = jnp.sum(crecv[0], axis=0)
 
     @pl.when(top)
     def _():
+        start_rows()
+        finish(0)
+
+    send_c3(1)
+
+    @pl.when(top)
+    def _():
         send_b3(0, own_pair[0])
+        send_b1(1, own_pair[1])
+
+    @pl.when(late_pair)
+    def _():
+        send_b1(0, own_pair[1])
+
+    @pl.when(jnp.logical_not(top))
+    def _():
+        start_rows()
+        older_left_terms(0, acc)
+        newest_left_term(0, acc)
+        finish(0)
 
     for j in range(1, FIRST):
         pend[j] = jnp.sum(crecv[j], axis=0)
@@ -460,13 +467,9 @@
                 psum[...] += right_term(l, j + 1)
             older_left_terms(j + 1, pend.at[j + 1])
         if j >= 1:
-            start_last(j - 1)
+            exchange(j - 1)
         if j >= 2:
-            exchange(j - 2)
-        if j >= 3:
-            last_product(j - 3)
-        if last:
-            exchange(j - 1)
+            last_product(j - 2)
         if j == 2:
             pl.when(late_pair)(functools.partial(send_b3, 0, own_pair[1]))
 
@@ -480,10 +483,8 @@
             acc[...] = pend[j + 1] - jnp.sum(brecv[j + 1], axis=0)
             finish(j + 1)
 
-    start_last(CB - 1)
-    last_product(CB - 3)
+    exchange(CB - 1)
     last_product(CB - 2)
-    exchange(CB - 1)
     last_product(CB - 1)
 
     for n in range(PAIRS):
@@ -499,8 +500,7 @@
         wait(crecv.at[blocks[c], pl.ds(0, nz - 1)], c3_send[c])
     for j in range(CB):
         wait(yx.at[j, pl.ds(0, nz - 1)], z_send[j])
-        wait(wrecv.at[j, pl.ds(0, nx - 1)], v_send[j])
-        wait(wbuf.at[j, :, pl.ds(0, (ns - 1) * ew)], w_send[j])
+        wait(at.at[0, pl.ds(0, (nx * ns - 1) * fw)], w_send[j])
         if j > 0:
             wait(brecv.at[j, pl.ds(0, nx - 1)], x_send[j])
         for k in range(1, RB):
@@ -580,9 +580,7 @@
         (CB, nx, fw, ew),
         (CB, nx, fw, ew),
         (CB, nx, fw, ew),
-        (CB, nx, fw, ew),
-        (CB, fw, ew),
-        (CB, fw, bs),
+        (CB, nx, fw, bs),
         (RB - 1, CB, fw, bs),
         (CB, fw, ew),
         (nx * fw, ew),

time: 118 us -> 114 us (0.966)
  Pallas kernels: 116 us -> 113 us
    pallas_call x1, Pallas kernels: 116 us -> 113 us  [shards(): pl.pallas_call(functools.partial(kernel, np_, nq), out_shape=jax.ShapeDty...]
where the time goes in v7:
time: 114 us
  Pallas kernels  113 us (99%)
  local copies, waits for them, and re-layouts  1.42 us (1%)
    pallas_call x1, Pallas kernels, shards(): pl.pallas_call(functools.partial(kernel, np_, nq), out_shape=jax.ShapeDty...  113 us

profile of v7, /device:TPU:1, one launch (start us, length us, event | category | flops | bytes accessed | tf_op | source)
XLA Modules:
  0.0 114.1 jit_solution(6387111682694014947)
XLA Ops:
  0.0 112.7 %shard_map.73 = f32[6,16,128]{2,1,0:T(8,128)} custom-call(f32[6,16,128]{2,1,0:T(8,128)} %refs_0_.1, f32[64,128]{1,0:T(8,128)} %bitcast.1, f32[128,512]{1,0:T(8,128)} %refs_2_.1, f32[4,512]{1,0:T(4,128)} %refs_3_.1, f32[6,16,512]{2,1,0:T(8,128)} %refs_4_.1, f32[6,512]{1,0:T(8,128)} %refs_5_.1, f32[6,16,3072]{2,1,0:T(8,128)} %refs_6_.1), custom_call_target="tpu_custom_call" | custom-call | tf_op jit(solution)/shard_map/pallas_call | solution.py:590
  112.7 1.4 %copy.9 = f32[6,16,128]{2,1,0:T(8,128)} copy(f32[6,16,128]{2,1,0:T(8,128)} %shard_map.73) | data formatting | bytes 98304

commit v8 on v7

--- a/solution.py
+++ b/solution.py
@@ -424,28 +424,24 @@
         wait(crecv.at[blocks[0]], c3_recv[0], "c3_0")
         acc[...] = jnp.sum(crecv[0], axis=0)
 
+    start_rows()
+    older_left_terms(0, acc)
+    newest_left_term(0, acc)
+    finish(0)
+
     @pl.when(top)
     def _():
-        start_rows()
-        finish(0)
+        send_b1(1, own_pair[1])
 
     send_c3(1)
 
     @pl.when(top)
     def _():
         send_b3(0, own_pair[0])
-        send_b1(1, own_pair[1])
 
     @pl.when(late_pair)
     def _():
         send_b1(0, own_pair[1])
-
-    @pl.when(jnp.logical_not(top))
-    def _():
-        start_rows()
-        older_left_terms(0, acc)
-        newest_left_term(0, acc)
-        finish(0)
 
     for j in range(1, FIRST):
         pend[j] = jnp.sum(crecv[j], axis=0)
@@ -455,9 +451,6 @@
         if j == 1:
             pl.when(top)(functools.partial(send_b2, 1))
             pl.when(late_pair)(functools.partial(send_b2, 0))
-            wait(crecv.at[blocks[1]], c3_recv[1], "c3_1")
-            for later in range(FIRST, CB):
-                pend[later] = jnp.sum(crecv[later], axis=0)
         if j == 2:
             pl.when(top)(functools.partial(send_b3, 1, own_pair[1]))
         if not last:
@@ -465,7 +458,8 @@
             psum[...] = jnp.zeros_like(psum)
             for l in range(j):
                 psum[...] += right_term(l, j + 1)
-            older_left_terms(j + 1, pend.at[j + 1])
+            if j + 1 != FIRST:
+                older_left_terms(j + 1, pend.at[j + 1])
         if j >= 1:
             exchange(j - 1)
         if j >= 2:
@@ -478,6 +472,11 @@
             xpart[j + 1] = (psum[...] + right_term(j, j + 1)).reshape(nx, fw, ew)
             scatter_x(xpart.at[j + 1], brecv.at[j + 1], x_send[j + 1], x_recv[j + 1])
             brecv[j + 1, x] = xpart[j + 1, x]
+            if j + 1 == FIRST:
+                wait(crecv.at[blocks[1]], c3_recv[1], "c3_1")
+                for later in range(FIRST, CB):
+                    pend[later] = jnp.sum(crecv[later], axis=0)
+                older_left_terms(j + 1, pend.at[j + 1])
             newest_left_term(j + 1, pend.at[j + 1])
             wait(brecv.at[j + 1, pl.ds(0, nx - 1)], x_recv[j + 1], "x_%d" % (j + 1))
             acc[...] = pend[j + 1] - jnp.sum(brecv[j + 1], axis=0)

time: 114 us -> 116 us (1.018)
    pallas_call x1, Pallas kernels: 113 us -> 114 us  [shards(): pl.pallas_call(functools.partial(kernel, np_, nq), out_shape=jax.ShapeDty...]
where the time goes in v8:
time: 116 us
  Pallas kernels  114 us (98%)
  local copies, waits for them, and re-layouts  1.42 us (1%)
    pallas_call x1, Pallas kernels, shards(): pl.pallas_call(functools.partial(kernel, np_, nq), out_shape=jax.ShapeDty...  114 us

profile of v8, /device:TPU:1, one launch (start us, length us, event | category | flops | bytes accessed | tf_op | source)
XLA Modules:
  0.0 115.7 jit_solution(8902546309525165300)
XLA Ops:
  0.0 114.3 %shard_map.73 = f32[6,16,128]{2,1,0:T(8,128)} custom-call(f32[6,16,128]{2,1,0:T(8,128)} %refs_0_.1, f32[64,128]{1,0:T(8,128)} %bitcast.1, f32[128,512]{1,0:T(8,128)} %refs_2_.1, f32[4,512]{1,0:T(4,128)} %refs_3_.1, f32[6,16,512]{2,1,0:T(8,128)} %refs_4_.1, f32[6,512]{1,0:T(8,128)} %refs_5_.1, f32[6,16,3072]{2,1,0:T(8,128)} %refs_6_.1), custom_call_target="tpu_custom_call" | custom-call | tf_op jit(solution)/shard_map/pallas_call | solution.py:589
  114.3 1.4 %copy.9 = f32[6,16,128]{2,1,0:T(8,128)} copy(f32[6,16,128]{2,1,0:T(8,128)} %shard_map.73) | data formatting | bytes 98304

commit v9 on v8

--- a/solution.py
+++ b/solution.py
@@ -450,7 +450,6 @@
         last = j + 1 == CB
         if j == 1:
             pl.when(top)(functools.partial(send_b2, 1))
-            pl.when(late_pair)(functools.partial(send_b2, 0))
         if j == 2:
             pl.when(top)(functools.partial(send_b3, 1, own_pair[1]))
         if not last:
@@ -464,14 +463,16 @@
             exchange(j - 1)
         if j >= 2:
             last_product(j - 2)
-        if j == 2:
-            pl.when(late_pair)(functools.partial(send_b3, 0, own_pair[1]))
 
         wait(yx.at[j, pl.ds(0, nz - 1)], z_recv[j], "z_%d" % j)
         if not last:
             xpart[j + 1] = (psum[...] + right_term(j, j + 1)).reshape(nx, fw, ew)
             scatter_x(xpart.at[j + 1], brecv.at[j + 1], x_send[j + 1], x_recv[j + 1])
             brecv[j + 1, x] = xpart[j + 1, x]
+            if j == 1:
+                pl.when(late_pair)(functools.partial(send_b2, 0))
+            if j == 2:
+                pl.when(late_pair)(functools.partial(send_b3, 0, own_pair[1]))
             if j + 1 == FIRST:
                 wait(crecv.at[blocks[1]], c3_recv[1], "c3_1")
                 for later in range(FIRST, CB):

time: 116 us -> 115 us (level)
    pallas_call x1, Pallas kernels: 114 us -> 113 us  [shards(): pl.pallas_call(functools.partial(kernel, np_, nq), out_shape=jax.ShapeDty...]
where the time goes in v9:
time: 115 us
  Pallas kernels  113 us (98%)
  local copies, waits for them, and re-layouts  1.42 us (1%)
    pallas_call x1, Pallas kernels, shards(): pl.pallas_call(functools.partial(kernel, np_, nq), out_shape=jax.ShapeDty...  113 us

profile of v9, /device:TPU:1, one launch (start us, length us, event | category | flops | bytes accessed | tf_op | source)
XLA Modules:
  0.0 114.5 jit_solution(15140910562556494151)
XLA Ops:
  0.0 113.1 %shard_map.73 = f32[6,16,128]{2,1,0:T(8,128)} custom-call(f32[6,16,128]{2,1,0:T(8,128)} %refs_0_.1, f32[64,128]{1,0:T(8,128)} %bitcast.1, f32[128,512]{1,0:T(8,128)} %refs_2_.1, f32[4,512]{1,0:T(4,128)} %refs_3_.1, f32[6,16,512]{2,1,0:T(8,128)} %refs_4_.1, f32[6,512]{1,0:T(8,128)} %refs_5_.1, f32[6,16,3072]{2,1,0:T(8,128)} %refs_6_.1), custom_call_target="tpu_custom_call" | custom-call | tf_op jit(solution)/shard_map/pallas_call | solution.py:590
  113.1 1.4 %copy.9 = f32[6,16,128]{2,1,0:T(8,128)} copy(f32[6,16,128]{2,1,0:T(8,128)} %shard_map.73) | data formatting | bytes 98304

commit v10 on v8

--- a/solution.py
+++ b/solution.py
@@ -433,15 +433,15 @@
     def _():
         send_b1(1, own_pair[1])
 
+    @pl.when(late_pair)
+    def _():
+        send_b1(0, own_pair[1])
+
     send_c3(1)
 
     @pl.when(top)
     def _():
         send_b3(0, own_pair[0])
-
-    @pl.when(late_pair)
-    def _():
-        send_b1(0, own_pair[1])
 
     for j in range(1, FIRST):
         pend[j] = jnp.sum(crecv[j], axis=0)
@@ -450,7 +450,6 @@
         last = j + 1 == CB
         if j == 1:
             pl.when(top)(functools.partial(send_b2, 1))
-            pl.when(late_pair)(functools.partial(send_b2, 0))
         if j == 2:
             pl.when(top)(functools.partial(send_b3, 1, own_pair[1]))
         if not last:
@@ -464,6 +463,9 @@
             exchange(j - 1)
         if j >= 2:
             last_product(j - 2)
+
+        if j == 1:
+            pl.when(late_pair)(functools.partial(send_b2, 0))
         if j == 2:
             pl.when(late_pair)(functools.partial(send_b3, 0, own_pair[1]))
 

time: 116 us -> 115 us (level)
  no operation moved by 1% of the time
where the time goes in v10:
time: 115 us
  Pallas kernels  113 us (98%)
  local copies, waits for them, and re-layouts  1.42 us (1%)
    pallas_call x1, Pallas kernels, shards(): pl.pallas_call(functools.partial(kernel, np_, nq), out_shape=jax.ShapeDty...  113 us

profile of v10, /device:TPU:1, one launch (start us, length us, event | category | flops | bytes accessed | tf_op | source)
XLA Modules:
  0.0 114.7 jit_solution(12687067805328609174)
XLA Ops:
  0.0 113.3 %shard_map.73 = f32[6,16,128]{2,1,0:T(8,128)} custom-call(f32[6,16,128]{2,1,0:T(8,128)} %refs_0_.1, f32[64,128]{1,0:T(8,128)} %bitcast.1, f32[128,512]{1,0:T(8,128)} %refs_2_.1, f32[4,512]{1,0:T(4,128)} %refs_3_.1, f32[6,16,512]{2,1,0:T(8,128)} %refs_4_.1, f32[6,512]{1,0:T(8,128)} %refs_5_.1, f32[6,16,3072]{2,1,0:T(8,128)} %refs_6_.1), custom_call_target="tpu_custom_call" | custom-call | tf_op jit(solution)/shard_map/pallas_call | solution.py:591
  113.3 1.4 %copy.9 = f32[6,16,128]{2,1,0:T(8,128)} copy(f32[6,16,128]{2,1,0:T(8,128)} %shard_map.73) | data formatting | bytes 98304

commit v11 on v9

--- a/solution.py
+++ b/solution.py
@@ -459,7 +459,7 @@
                 psum[...] += right_term(l, j + 1)
             if j + 1 != FIRST:
                 older_left_terms(j + 1, pend.at[j + 1])
-        if j >= 1:
+        if last:
             exchange(j - 1)
         if j >= 2:
             last_product(j - 2)
@@ -469,6 +469,8 @@
             xpart[j + 1] = (psum[...] + right_term(j, j + 1)).reshape(nx, fw, ew)
             scatter_x(xpart.at[j + 1], brecv.at[j + 1], x_send[j + 1], x_recv[j + 1])
             brecv[j + 1, x] = xpart[j + 1, x]
+            if j >= 1:
+                exchange(j - 1)
             if j == 1:
                 pl.when(late_pair)(functools.partial(send_b2, 0))
             if j == 2:

time: 115 us -> 115 us (level)
  no operation moved by 1% of the time
where the time goes in v11:
time: 115 us
  Pallas kernels  113 us (98%)
  local copies, waits for them, and re-layouts  1.42 us (1%)
    pallas_call x1, Pallas kernels, shards(): pl.pallas_call(functools.partial(kernel, np_, nq), out_shape=jax.ShapeDty...  113 us

profile of v11, /device:TPU:1, one launch (start us, length us, event | category | flops | bytes accessed | tf_op | source)
XLA Modules:
  0.0 114.8 jit_solution(11536922834482085380)
XLA Ops:
  0.0 113.4 %shard_map.73 = f32[6,16,128]{2,1,0:T(8,128)} custom-call(f32[6,16,128]{2,1,0:T(8,128)} %refs_0_.1, f32[64,128]{1,0:T(8,128)} %bitcast.1, f32[128,512]{1,0:T(8,128)} %refs_2_.1, f32[4,512]{1,0:T(4,128)} %refs_3_.1, f32[6,16,512]{2,1,0:T(8,128)} %refs_4_.1, f32[6,512]{1,0:T(8,128)} %refs_5_.1, f32[6,16,3072]{2,1,0:T(8,128)} %refs_6_.1), custom_call_target="tpu_custom_call" | custom-call | tf_op jit(solution)/shard_map/pallas_call | solution.py:592
  113.4 1.4 %copy.9 = f32[6,16,128]{2,1,0:T(8,128)} copy(f32[6,16,128]{2,1,0:T(8,128)} %shard_map.73) | data formatting | bytes 98304
